TPU v7x, 128 devices: a whole 4x4x4 slice. The times are simulated.
128 devices in a mesh: ep: 32 (over x, z, core), tp: 4 (over y).
Axes of the slice: x: 4, y: 4, z: 4, core: 2. Of those that a mesh axis runs over, the one named last changes fastest.
Arguments:
- cache_pages: bfloat16 [2048, 256, 576], P(('ep', 'tp')), may hold values from -6 to 6
- queries: bfloat16 [2048, 128, 576], P(('ep', 'tp')), may hold values from -400 to 400
- lengths: int32 [2048], replicated, may hold values from 2 to 256, as said below
- swap_slot: int32 [128], replicated, may hold values from 0 to 15
- swap_mask: int32 [1], replicated, may hold values from 1 to 31
- hidden: bfloat16 [2048, 3584], P('ep'), may hold values from -6 to 6
- expert_ids: int32 [2048, 8], P('ep'), may hold values from 0 to 95, all different within a row; in each aligned block of 64 rows (0 to 63, 64 to 127, ...) at most 10 rows name the same one
- gate_weights: float32 [2048, 8], P('ep'), may hold values from 0.1 to 0.6
- w_gate: bfloat16 [96, 3584, 1024], P('ep', None, 'tp'), may hold values from -0.09375 to 0.09375
- w_up: bfloat16 [96, 3584, 1024], P('ep', None, 'tp'), may hold values from -0.09375 to 0.09375
- w_down: bfloat16 [96, 1024, 3584], P('ep', 'tp'), may hold values from -0.1875 to 0.1875
Outputs:
- attention_out: bfloat16 [2048, 128, 512], P(('ep', 'tp'))
- moe_out: bfloat16 [2048, 3584], P('ep', 'tp')
Inputs may be any that keep to these rules, and one draw needn't show every extreme that they name: `lengths`: each request's cache holds at least 2 tokens; some request holds exactly 256. `expert_ids`: A row's 8 experts are distinct. Among the 64 rows of one ep rank no expert is named by more than 10 rows, a bound that some block reaches.
All inputs are finite; a program needn't handle non-finite values.
Results may differ from a plain program's by a relative error of at most 0.012.
Values may be sent and summed in bfloat16 or wider, within the bound.
A program may use at most 128 MiB of HBM per device.

v0:
```python
import jax
import jax.numpy as jnp
from jax import lax
from jax.sharding import PartitionSpec as P

LAT = 512


SCORE_SCALE = 192.0 ** (-0.5)
MASK_FLOOR = -1e30


def from_partner(block, axis, apart):
    count = lax.axis_size(axis)
    route = []
    for low in range(count):
        high = low | 1 << apart
        if high != low and high < count:
            route += [(low, high), (high, low)]
    return lax.ppermute(block, axis, route)


def bit_chosen(mask_value, bit_level):
    return jnp.bitwise_and(jnp.right_shift(mask_value, bit_level), 1) == 1


def apply_sections(payload, mask_value, sections, section_move):
    for bit_level in range(sections):
        chosen_bit = bit_chosen(mask_value, bit_level)
        swapped = section_move(payload, bit_level)
        payload = jnp.where(chosen_bit, swapped, payload)
    return payload


def page_section(payload, bit_level):
    return from_partner(payload, "ep", bit_level)


def attend_local(asked_rows, keys_vals, live_lengths):
    scores = (
        jnp.einsum("rhk,rpk->rhp", asked_rows, keys_vals, preferred_element_type=jnp.float32)
        * SCORE_SCALE
    )
    live_mask = (
        jnp.arange(keys_vals.shape[1], dtype=jnp.int32)[None, None, :] < live_lengths[:, None, None]
    )
    scores = jnp.where(live_mask, scores, MASK_FLOOR)
    highest = jnp.max(scores, axis=2, keepdims=True)
    weight = jnp.where(live_mask, jnp.exp(scores - highest), 0.0)
    totals = jnp.sum(weight, axis=2, keepdims=True)
    weight_low = weight.astype(jnp.bfloat16)
    blended = jnp.einsum(
        "rhp,rpd->rhd", weight_low, keys_vals[:, :, :LAT], preferred_element_type=jnp.float32
    )
    return (blended / totals).astype(jnp.bfloat16)


def local(
    cache_pages,
    queries,
    lengths,
    swap_slot,
    swap_mask,
    hidden,
    expert_ids,
    gate_weights,
    w_gate,
    w_up,
    w_down,
):
    local_count = cache_pages.shape[0]
    groups = lax.axis_size("tp")
    ep_rank = lax.axis_index("ep")
    tp_rank = lax.axis_index("tp")
    device = ep_rank * groups + tp_rank
    mask_value = swap_mask[0]
    partner = jnp.bitwise_xor(ep_rank, mask_value) * groups + tp_rank
    my_slot = swap_slot[device]
    far_slot = swap_slot[partner]
    sections = lax.axis_size("ep").bit_length() - 1
    own_lengths = lax.dynamic_slice_in_dim(lengths, device * local_count, local_count)
    slot_range = jnp.arange(local_count, dtype=jnp.int32)
    own_page = lax.dynamic_index_in_dim(cache_pages, my_slot, 0, keepdims=False)
    arrived = apply_sections(own_page, mask_value, sections, page_section)
    keys_vals = lax.dynamic_update_index_in_dim(cache_pages, arrived, my_slot, 0)
    live_lengths = jnp.where(
        slot_range == my_slot, lengths[partner * local_count + far_slot], own_lengths
    )
    attended = attend_local(queries, keys_vals, live_lengths)
    rows_count = hidden.shape[0]
    top_count = expert_ids.shape[1]
    expert_local = w_gate.shape[0]
    ep_size = lax.axis_size("ep")
    experts_all = ep_size * expert_local
    capacity = max(2, 2 * rows_count * top_count // experts_all)
    model_width = hidden.shape[1]
    flat_ids = expert_ids.reshape(-1)
    onehot = (flat_ids[:, None] == jnp.arange(experts_all, dtype=jnp.int32)[None, :]).astype(
        jnp.int32
    )
    pair_rank = jnp.sum(jnp.cumsum(onehot, axis=0) * onehot, axis=1) - 1
    slot_ids = flat_ids * capacity + pair_rank
    select = (
        slot_ids[None, :] == jnp.arange(experts_all * capacity, dtype=jnp.int32)[:, None]
    ).reshape(experts_all * capacity, rows_count, top_count)
    picker = jnp.any(select, axis=2).astype(jnp.bfloat16)
    pick_table = select.astype(jnp.bfloat16)
    outgoing = jnp.dot(picker, hidden, preferred_element_type=jnp.float32).astype(jnp.bfloat16)
    outgoing = outgoing.reshape(ep_size, expert_local, capacity, model_width)
    block_rows = lax.all_to_all(outgoing, "ep", split_axis=0, concat_axis=0, tiled=True)
    gate_act = jnp.einsum("sejd,edf->sejf", block_rows, w_gate, preferred_element_type=jnp.float32)
    up_act = jnp.einsum("sejd,edf->sejf", block_rows, w_up, preferred_element_type=jnp.float32)
    inner_act = (jax.nn.silu(gate_act) * up_act).astype(jnp.bfloat16)
    partials = jnp.einsum(
        "sejf,efd->sejd", inner_act, w_down, preferred_element_type=jnp.float32
    ).astype(jnp.bfloat16)
    returned = lax.all_to_all(partials, "ep", split_axis=0, concat_axis=0, tiled=True)
    summed = lax.psum_scatter(
        returned.reshape(experts_all * capacity, model_width)
        .astype(jnp.float32)
        .astype(jnp.bfloat16),
        "tp",
        scatter_dimension=1,
        tiled=True,
    )
    picked = jnp.einsum("srk,sd->rkd", pick_table, summed, preferred_element_type=jnp.float32)
    moe_rows = jnp.sum(picked * gate_weights[:, :, None], axis=1)
    return (attended, moe_rows.astype(jnp.bfloat16))


def solution(mesh):
    in_specs = (
        P(("ep", "tp"), None, None),
        P(("ep", "tp"), None, None),
        P(),
        P(),
        P(),
        P("ep", None),
        P("ep", None),
        P("ep", None),
        P("ep", None, "tp"),
        P("ep", None, "tp"),
        P("ep", "tp", None),
    )
    out_specs = (P(("ep", "tp"), None, None), P("ep", "tp"))
    return jax.shard_map(local, mesh=mesh, in_specs=in_specs, out_specs=out_specs, check_vma=False)
```

profile of v0, /device:TPU:1, one launch (start us, length us, event | category | flops | bytes accessed | tf_op | source)
XLA Modules:
  0.0 406.2 jit_solution(6477426547376618994)
XLA Ops:
  11.7 5.8 %convolution_convert_fusion = bf16[960,3584]{1,0:T(8,128)(2,1)} fusion(pred[960,64]{0,1:T(8,128)(4,1)S(1)} %fusion.15, bf16[64,3584]{1,0:T(8,128)(2,1)} %param.16), kind=kOutput, calls=%fused_computation.1 | convolution fusion | flops 443842560 | bytes 7401472 | tf_op jit(solution)/shard_map/dot_general | solution.py:108
  17.6 11.0 %reshape.73 = bf16[32,3,10,3584]{3,2,1,0:T(8,128)(2,1)} reshape(bf16[960,3584]{1,0:T(8,128)(2,1)} %convolution_convert_fusion) | data formatting | bytes 13762560 | tf_op jit(solution)/shard_map/reshape | solution.py:109
  28.5 9.8 %copy.69 = bf16[32,3,10,3584]{3,1,2,0:T(4,128)(2,1)S(1)} copy(bf16[32,3,10,3584]{3,2,1,0:T(8,128)(2,1)} %reshape.73) | data formatting | bytes 13762560 | tf_op jit(solution)/shard_map/reshape | solution.py:109
  38.4 113.3 %all_to_all.10 = bf16[32,3,10,3584]{3,1,2,0:T(4,128)(2,1)S(1)} all-to-all(bf16[32,3,10,3584]{3,1,2,0:T(4,128)(2,1)S(1)} %copy.69), channel_id=1, replica_groups=mesh['ep'=32,'tp'=4] {'ep'}, dimensions={0} | all-to-all | bytes 13762560 | tf_op jit(solution)/shard_map/all_to_all | solution.py:110
  151.7 3.5 copy-done.1
  155.2 6.6 %fusion.23 = f32[32,3,10,256]{3,0,2,1:T(8,128)S(1)} fusion(bf16[3,3584,256]{2,1,0:T(8,128)(2,1)} %param.19, bf16[32,3,10,3584]{3,1,2,0:T(4,128)(2,1)S(1)} %all_to_all.10), kind=kOutput, calls=%fused_computation.25 | convolution fusion | flops 1761607680 | bytes 13369344 | tf_op jit(solution)/shard_map/sejd,edf->sejf/dot_general | solution.py:111
  161.9 14.2 %fusion.1 = bf16[32,3,10,3584]{3,0,2,1:T(8,128)(2,1)} fusion(bf16[3,256,3584]{2,1,0:T(8,128)(2,1)} %param.21, bf16[3,3584,256]{2,1,0:T(8,128)(2,1)} %param.20, bf16[32,3,10,3584]{3,1,2,0:T(4,128)(2,1)} %copy-done.1, f32[32,3,10,256]{3,0,2,1:T(8,128)S(1)} %fusion.23), kind=kOutput, calls=%fused_computation.3 | convolution fusion | flops 3528130560 | bytes 25755648 | tf_op jit(solution)/shard_map/sejf,efd->sejd/dot_general | solution.py:114
  176.1 9.1 %copy.72 = bf16[32,3,10,3584]{3,1,2,0:T(4,128)(2,1)S(1)} copy(bf16[32,3,10,3584]{3,0,2,1:T(8,128)(2,1)} %fusion.1) | data formatting | bytes 13762560 | tf_op jit(solution)/shard_map/convert_element_type | solution.py:116
  185.2 107.8 %all_to_all.11 = bf16[32,3,10,3584]{3,1,2,0:T(4,128)(2,1)} all-to-all(bf16[32,3,10,3584]{3,1,2,0:T(4,128)(2,1)S(1)} %copy.72), channel_id=1, replica_groups=mesh['ep'=32,'tp'=4] {'ep'}, dimensions={0} | all-to-all | bytes 13762560 | tf_op jit(solution)/shard_map/all_to_all | solution.py:117
  293.0 10.8 %copy.73 = bf16[32,3,10,3584]{3,2,1,0:T(8,128)(2,1)} copy(bf16[32,3,10,3584]{3,1,2,0:T(4,128)(2,1)} %all_to_all.11) | data formatting | bytes 13762560 | tf_op jit(solution)/shard_map/all_to_all | solution.py:117
  303.8 11.3 %reshape.74 = bf16[960,3584]{1,0:T(8,128)(2,1)} reshape(bf16[32,3,10,3584]{3,2,1,0:T(8,128)(2,1)} %copy.73) | data formatting | bytes 13762560 | tf_op jit(solution)/shard_map/reshape | solution.py:119
  315.1 10.3 %copy.80 = bf16[960,3584]{0,1:T(8,128)(2,1)} copy(bf16[960,3584]{1,0:T(8,128)(2,1)} %reshape.74) | data formatting | bytes 13762560
  330.1 1.6 collective-permute-done
  331.8 9.2 %collective-permute-done.1 = bf16[256,576]{1,0:T(8,128)(2,1)S(1)} collective-permute-done((bf16[256,576]{1,0:T(8,128)(2,1)S(1)}, bf16[256,576]{1,0:T(8,128)(2,1)S(1)}, u32[]{:S(2)}, u32[]{:S(2)}) %collective-permute-start.1) | collective-permute-done | bytes 294944 | tf_op jit(solution)/shard_map/ppermute | solution.py:20
  342.1 9.0 %collective-permute-done.2 = bf16[256,576]{1,0:T(8,128)(2,1)S(1)} collective-permute-done((bf16[256,576]{1,0:T(8,128)(2,1)S(1)}, bf16[256,576]{1,0:T(8,128)(2,1)S(1)}, u32[]{:S(2)}, u32[]{:S(2)}) %collective-permute-start.2) | collective-permute-done | bytes 294944 | tf_op jit(solution)/shard_map/ppermute | solution.py:20
  351.2 7.8 %copy.61 = bf16[16,256,576]{2,1,0:T(8,128)(2,1)} copy(bf16[16,256,576]{1,2,0:T(8,128)(2,1)} %param.11) | data formatting | bytes 9437184 | tf_op args[0]
  359.8 1.3 dynamic_slice.18
  361.1 1.7 collective-permute-start.4
  362.8 2.1 compare_select_fusion
  364.9 5.2 %collective-permute-done.4 = bf16[256,576]{1,0:T(8,128)(2,1)S(1)} collective-permute-done((bf16[256,576]{1,0:T(8,128)(2,1)S(1)}, bf16[256,576]{1,0:T(8,128)(2,1)S(1)}, u32[]{:S(2)}, u32[]{:S(2)}) %collective-permute-start.4) | collective-permute-done | bytes 294944 | tf_op jit(solution)/shard_map/ppermute | solution.py:20
  371.0 4.6 %fusion.65 = (f32[16,128]{1,0:T(8,128)S(1)}, bf16[16,128,256]{1,2,0:T(8,128)(2,1)}) fusion(pred[16,256]{1,0:T(8,128)(4,1)S(1)} %iota_compare_fusion.6, bf16[16,256,576]{2,1,0:T(8,128)(2,1)} %bitcast_dynamic-update-slice_fusion, bf16[16,128,576]{1,2,0:T(8,128)(2,1)S(1)} %copy-done), kind=kOutput, calls=%fused_computation.62 | convolution fusion | flops 607125760 | bytes 8138752 | tf_op jit(solution)/shard_map/sub | solution.py:49
  375.6 4.7 %divide_convert_fusion = bf16[16,128,512]{2,1,0:T(8,128)(2,1)} fusion(f32[16,128]{1,0:T(8,128)S(1)} %get-tuple-element.4, bf16[16,256,576]{2,1,0:T(8,128)(2,1)} %bitcast_dynamic-update-slice_fusion, bf16[16,128,256]{1,2,0:T(8,128)(2,1)} %get-tuple-element.5), kind=kOutput, calls=%fused_computation.13 | convolution fusion | flops 538968064 | bytes 7348224 | tf_op jit(solution)/shard_map/rhp,rpd->rhd/dot_general | solution.py:52
  380.2 15.4 %reduce-scatter.4.cloned.1.call-done = bf16[896,960]{1,0:T(8,128)(2,1)} async-done(((bf16[3584,960]{1,0:T(8,128)(2,1)}), bf16[896,960]{1,0:T(8,128)(2,1)}) %reduce-scatter.4.cloned.1.call-update) | async-done | bytes 1720336
  395.7 3.7 multiply_reduce_fusion
  (39 shorter events, 8.7 us)
Async XLA Ops:
  7.2 363.8 %copy-start = (bf16[16,128,576]{1,2,0:T(8,128)(2,1)S(1)}, bf16[16,128,576]{1,2,0:T(8,128)(2,1)}, u32[]{:S(2)}) copy-start(bf16[16,128,576]{1,2,0:T(8,128)(2,1)} %param.12) | copy-start | bytes 7077892
  7.2 388.5 %reduce-scatter.4.cloned.1.call-start = ((), (), s32[]{:S(2)}) async-start(), calls=%async_computation.3 | async-start | bytes 9175040
  151.7 3.5 copy-start.1
  325.4 0.7 copy-start.3
  330.0 1.7 collective-permute-start
  331.7 9.3 %collective-permute-start.1 = (bf16[256,576]{1,0:T(8,128)(2,1)S(1)}, bf16[256,576]{1,0:T(8,128)(2,1)S(1)}, u32[]{:S(2)}, u32[]{:S(2)}) collective-permute-start(bf16[256,576]{1,0:T(8,128)(2,1)S(1)} %broadcast_select_fusion), channel_id=1, source_target_pairs={{0,8},{8,0},{4,12},{12,4},{16,24},{24,16},{20,28},{28,20},{32,40},... | collective-permute-start | bytes 884744 | tf_op jit(solution)/shard_map/ppermute | solution.py:20
  341.1 10.0 %collective-permute-start.2 = (bf16[256,576]{1,0:T(8,128)(2,1)S(1)}, bf16[256,576]{1,0:T(8,128)(2,1)S(1)}, u32[]{:S(2)}, u32[]{:S(2)}) collective-permute-start(bf16[256,576]{1,0:T(8,128)(2,1)S(1)} %broadcast_select_fusion.1), channel_id=1, source_target_pairs={{0,16},{16,0},{4,20},{20,4},{8,24},{24,8},{12,28},{28,12},{32,48},... | collective-permute-start | bytes 884744 | tf_op jit(solution)/shard_map/ppermute | solution.py:20
  351.1 8.6 %copy-start.2 = (f32[64,8]{0,1:T(8,128)S(1)}, f32[64,8]{0,1:T(8,128)}, u32[]{:S(2)}) copy-start(f32[64,8]{0,1:T(8,128)} %param.18) | copy-start | bytes 6148
  351.1 9.9 %collective-permute-start.3 = (bf16[256,576]{1,0:T(8,128)(2,1)S(1)}, bf16[256,576]{1,0:T(8,128)(2,1)S(1)}, u32[]{:S(2)}, u32[]{:S(2)}) collective-permute-start(bf16[256,576]{1,0:T(8,128)(2,1)S(1)} %broadcast_select_fusion.2), channel_id=1, source_target_pairs={{0,32},{32,0},{4,36},{36,4},{8,40},{40,8},{12,44},{44,12},{16,48},... | collective-permute-start | bytes 884744 | tf_op jit(solution)/shard_map/ppermute | solution.py:20
  361.1 9.0 %collective-permute-start.4 = (bf16[256,576]{1,0:T(8,128)(2,1)S(1)}, bf16[256,576]{1,0:T(8,128)(2,1)S(1)}, u32[]{:S(2)}, u32[]{:S(2)}) collective-permute-start(bf16[256,576]{1,0:T(8,128)(2,1)S(1)} %broadcast_select_fusion.3), channel_id=1, source_target_pairs={{0,64},{64,0},{4,68},{68,4},{8,72},{72,8},{12,76},{76,12},{16,80},... | collective-permute-start | bytes 884744 | tf_op jit(solution)/shard_map/ppermute | solution.py:20
Sparse Core Ops, SparseCore 0:
  325.6 70.0 reduce-scatter.3
where the time goes:
time: 408 us; the launch traced here: 406 us
  blocking collectives  221 us (54%)
  local copies, waits for them, and re-layouts  78.5 us (19%)
  waiting for transfers between devices  40.5 us (10%)
  matrix products  39.6 us (10%)
  between operations  17.5 us (4%)
  other arithmetic  6.02 us (1%)
    all_to_all x1, blocking collectives, local(): lax.all_to_all(outgoing, 'ep', split_axis=0, concat_axis=0, tiled=True)  113 us
    all_to_all x1, blocking collectives, local(): lax.all_to_all(partials, 'ep', split_axis=0, concat_axis=0, tiled=True)  108 us
    ppermute x5, waiting for transfers between devices, from_partner(): return lax.ppermute(block, axis, route)  25 us
    unnamed x12, local copies, waits for them, and re-layouts  22.6 us
    reshape x2, local copies, waits for them, and re-layouts, local(): outgoing = outgoing.reshape(ep_size, expert_local, capacity, model_width)  20.8 us
    unnamed x2, waiting for transfers between devices  15.4 us
    dot_general x1, matrix products, local(): jnp.einsum('sejf,efd->sejd', inner_act, w_down, preferred_element_type=jn...  14.2 us
    reshape x1, local copies, waits for them, and re-layouts, local(): returned.reshape(experts_all * capacity, model_width).astype(jnp.float32)  11.3 us
  transfers between devices with their start and end apart: 6, of which 5 were waited for; matrix products, arithmetic and copies ran while one was open for 6% of the time, Pallas kernels for 0%

commit v1 on v0

v1 whole, which is shorter than its diff:
```python
import functools

import jax
import jax.numpy as jnp
from jax import lax
from jax.experimental import pallas as pl
from jax.experimental.pallas import tpu as pltpu
from jax.sharding import PartitionSpec as P

MESH = pl.DeviceIdType.MESH
BF = jnp.bfloat16
F32 = jnp.float32
LAT = 512
D = 3584
ROWS = 64
CAP = 10
EXL = 3
META = 256
XW = D + META
GROUP = 512
GSLOT = 80
HALF = D // 2
BLK = D // 4
FFL = 256
SCORE_SCALE = 192.0 ** (-0.5)
MASK_FLOOR = -1e30
VMEM_MAX = 60 * 1024 * 1024


def coords():
    e = lax.axis_index("ep")
    return e // 8, lax.rem(e // 2, 4), lax.rem(e, 2), lax.axis_index("tp")


def wrap(v):
    return lax.rem(v + 4, 4)


def greet(targets):
    barrier = pltpu.get_barrier_semaphore()
    for target in targets:
        pl.semaphore_signal(barrier, inc=1, device_id=target, device_id_type=MESH)
    pl.semaphore_wait(barrier, len(targets))


def gather_kernel(x_ref, wd_ref, xg_ref, wdp_ref, ssem, rsem1, rsem2, dsend, drecv, wsem, lsem):
    x, z, c, y = coords()

    def dev(xx, zz, cc):
        return (xx * 8 + zz * 2 + cc, y)

    other = dev(x, z, 1 - c)
    greet([dev(wrap(x + 1), z, c), dev(wrap(x - 1), z, c), dev(x, wrap(z + 1), c), dev(x, wrap(z - 1), c), other])

    started = []
    count = [0, 0]

    def ship(col, src, dst, target, recv):
        copy = pltpu.make_async_remote_copy(
            src_ref=src,
            dst_ref=dst,
            send_sem=ssem.at[col, count[col]],
            recv_sem=recv,
            device_id=target,
            device_id_type=MESH,
        )
        count[col] += 1
        copy.start()
        started.append(copy)
        return copy

    first = (x, z)
    second = (z, x)

    def place(col, f, s, lo=0, size=32):
        xx, zz = (f, s) if col == 0 else (s, f)
        return xg_ref.at[xx, zz, c, pl.ds(col * 32 + lo, size)]

    def fdev(col, f):
        return dev(f, z, c) if col == 0 else dev(x, f, c)

    def sdev(col, s):
        return dev(x, s, c) if col == 0 else dev(s, z, c)

    def own(col):
        return x_ref.at[pl.ds(col * 32, 32)]

    def expect(ref, sem):
        pltpu.make_async_copy(ref, ref, sem).wait()

    def share(col, f, s, src=None):
        xx, zz = (f, s) if col == 0 else (s, f)
        slot = xx * 4 + zz
        ref = place(col, f, s)
        copy = pltpu.make_async_remote_copy(
            src_ref=ref if src is None else src,
            dst_ref=ref,
            send_sem=dsend.at[col, slot],
            recv_sem=drecv.at[col, slot],
            device_id=other,
            device_id_type=MESH,
        )
        copy.start()
        started.append(copy)

    def fan(col, k, f, src=None):
        s = second[col]
        ref = place(col, f, s)
        src = ref if src is None else src
        ship(col, src, ref, sdev(col, wrap(s + 1)), rsem2.at[col, k, 0])
        ship(col, src, ref, sdev(col, wrap(s - 1)), rsem2.at[col, k, 1])

    def relay2(col, k, f):
        s = second[col]
        back, ahead = place(col, f, wrap(s - 1)), place(col, f, wrap(s + 1))
        expect(back, rsem2.at[col, k, 0])
        ref = place(col, f, wrap(s - 1), 0, 16)
        ship(col, ref, ref, sdev(col, wrap(s + 1)), rsem2.at[col, k, 2])
        share(col, f, wrap(s - 1))
        expect(ahead, rsem2.at[col, k, 1])
        ref = place(col, f, wrap(s + 1), 16, 16)
        ship(col, ref, ref, sdev(col, wrap(s - 1)), rsem2.at[col, k, 3])
        share(col, f, wrap(s + 1))

    def last2(col, k, f):
        s = wrap(second[col] + 2)
        expect(place(col, f, s, 0, 16), rsem2.at[col, k, 2])
        expect(place(col, f, s, 16, 16), rsem2.at[col, k, 3])
        share(col, f, s)

    for col in (0, 1):
        p, s = first[col], second[col]
        ref = place(col, p, s)
        ship(col, own(col), ref, fdev(col, wrap(p + 1)), rsem1.at[col, 0])
        ship(col, own(col), ref, fdev(col, wrap(p - 1)), rsem1.at[col, 1])
    for col in (0, 1):
        fan(col, 0, first[col], own(col))
        share(col, first[col], second[col], own(col))
    local = pltpu.make_async_copy(x_ref, xg_ref.at[x, z, c], lsem)
    local.start()
    far = pl.ds(pl.multiple_of((1 - c) * HALF, HALF), HALF)
    weights = pltpu.make_async_remote_copy(
        src_ref=wd_ref.at[:, :, far],
        dst_ref=wdp_ref,
        send_sem=wsem.at[0],
        recv_sem=wsem.at[1],
        device_id=other,
        device_id_type=MESH,
    )
    weights.start()
    for col in (0, 1):
        p, s = first[col], second[col]
        expect(place(col, wrap(p - 1), s), rsem1.at[col, 0])
        ref = place(col, wrap(p - 1), s, 0, 16)
        ship(col, ref, ref, fdev(col, wrap(p + 1)), rsem1.at[col, 2])
        fan(col, 1, wrap(p - 1))
        share(col, wrap(p - 1), s)
        expect(place(col, wrap(p + 1), s), rsem1.at[col, 1])
        ref = place(col, wrap(p + 1), s, 16, 16)
        ship(col, ref, ref, fdev(col, wrap(p - 1)), rsem1.at[col, 3])
        fan(col, 2, wrap(p + 1))
        share(col, wrap(p + 1), s)
    for col in (0, 1):
        relay2(col, 0, first[col])
    for col in (0, 1):
        p, s = first[col], second[col]
        expect(place(col, wrap(p + 2), s, 0, 16), rsem1.at[col, 2])
        expect(place(col, wrap(p + 2), s, 16, 16), rsem1.at[col, 3])
        fan(col, 3, wrap(p + 2))
        share(col, wrap(p + 2), s)
    for col in (0, 1):
        relay2(col, 1, wrap(first[col] - 1))
        relay2(col, 2, wrap(first[col] + 1))
    for col in (0, 1):
        last2(col, 0, first[col])
    for col in (0, 1):
        relay2(col, 3, wrap(first[col] + 2))
    for col in (0, 1):
        last2(col, 1, wrap(first[col] - 1))
        last2(col, 2, wrap(first[col] + 1))
    for col in (0, 1):
        last2(col, 3, wrap(first[col] + 2))
    for col in (0, 1):
        for slot in range(16):
            expect(xg_ref.at[slot // 4, slot % 4, 1 - c, pl.ds(col * 32, 32)], drecv.at[col, slot])
    weights.wait_recv()
    for copy in started:
        copy.wait_send()
    weights.wait_send()
    local.wait()


def gather_rows(xin, w_down):
    return pl.pallas_call(
        gather_kernel,
        out_shape=(
            jax.ShapeDtypeStruct((4, 4, 2, ROWS, XW), BF),
            jax.ShapeDtypeStruct((EXL, FFL, HALF), BF),
        ),
        in_specs=[pl.BlockSpec(memory_space=pltpu.VMEM), pl.BlockSpec(memory_space=pl.ANY)],
        out_specs=(pl.BlockSpec(memory_space=pl.ANY), pl.BlockSpec(memory_space=pl.ANY)),
        scratch_shapes=[
            pltpu.SemaphoreType.DMA((2, 20)),
            pltpu.SemaphoreType.DMA((2, 4)),
            pltpu.SemaphoreType.DMA((2, 4, 4)),
            pltpu.SemaphoreType.DMA((2, 16)),
            pltpu.SemaphoreType.DMA((2, 16)),
            pltpu.SemaphoreType.DMA((2,)),
            pltpu.SemaphoreType.DMA,
        ],
        compiler_params=pltpu.CompilerParams(
            collective_id=0, has_side_effects=True, vmem_limit_bytes=VMEM_MAX
        ),
        name="gather_rows",
    )(xin, w_down)


def slot_numbers(shape, axis):
    s = lax.broadcasted_iota(jnp.int32, shape, axis)
    g = lax.broadcasted_iota(jnp.int32, shape, 1 - axis)
    expert = jnp.zeros(shape, jnp.int32)
    for k in range(1, shape[axis] // GSLOT):
        expert = expert + (s >= k * GSLOT).astype(jnp.int32)
    u = s - expert * GSLOT
    rank = (u * 205) >> 11
    want = jnp.where((g >> 6) == rank, u - rank * CAP + 1, -1)
    return want.astype(F32)


def expert_lanes(shape, axis, base):
    s = lax.broadcasted_iota(jnp.int32, shape, axis)
    e = lax.broadcasted_iota(jnp.int32, shape, 1 - axis)
    expert = jnp.zeros(shape, jnp.int32)
    for k in range(1, shape[axis] // GSLOT):
        expert = expert + (s >= k * GSLOT).astype(jnp.int32)
    return jnp.where(expert + base == e, 1.0, 0.0).astype(BF)


def up_kernel(base_ref, x_ref, wg_hbm, wu_hbm, out_ref, xc, want, lanes, wg, wu, sem):
    q = pl.program_id(0)
    gate_copy = pltpu.make_async_copy(wg_hbm, wg, sem.at[0])
    up_copy = pltpu.make_async_copy(wu_hbm, wu, sem.at[1])

    @pl.when(q == 0)
    def _():
        gate_copy.start()
        up_copy.start()
        want[...] = slot_numbers((EXL * GSLOT, GROUP), 0)
        lanes[...] = expert_lanes((EXL * GSLOT, 128), 0, base_ref[0])

    table = x_ref[0, :, D : D + 128]
    named = lax.dot_general(lanes[...], table, (((1,), (1,)), ((), ())), preferred_element_type=F32)
    pick = jnp.where(named == want[...], 1.0, 0.0).astype(BF)
    start = pl.multiple_of(q * GSLOT, 16)

    @pl.loop(0, D // 512)
    def _(n):
        cols = pl.ds(pl.multiple_of(n * 512, 512), 512)
        rows = jnp.dot(pick, x_ref[0, :, cols], preferred_element_type=F32).astype(BF)
        for e in range(EXL):
            xc[e, pl.ds(start, GSLOT), cols] = rows[e * GSLOT : (e + 1) * GSLOT]

    @pl.when(q == 3)
    def _():
        gate_copy.wait()
        up_copy.wait()

        @pl.loop(0, EXL)
        def _(e):
            gate = jnp.dot(xc[e], wg[e], preferred_element_type=F32)
            up = jnp.dot(xc[e], wu[e], preferred_element_type=F32)
            out_ref[e] = (gate / (1.0 + jnp.exp(-gate)) * up).astype(BF)


def experts_up(base, xg, w_gate, w_up):
    return pl.pallas_call(
        up_kernel,
        out_shape=jax.ShapeDtypeStruct((EXL, 4 * GSLOT, FFL), BF),
        grid_spec=pltpu.PrefetchScalarGridSpec(
            num_scalar_prefetch=1,
            grid=(4,),
            in_specs=[
                pl.BlockSpec((1, GROUP, XW), lambda q, b: (q, 0, 0)),
                pl.BlockSpec(memory_space=pl.ANY),
                pl.BlockSpec(memory_space=pl.ANY),
            ],
            out_specs=pl.BlockSpec((EXL, 4 * GSLOT, FFL), lambda q, b: (0, 0, 0)),
            scratch_shapes=[
                pltpu.VMEM((EXL, 4 * GSLOT, D), BF),
                pltpu.VMEM((EXL * GSLOT, GROUP), F32),
                pltpu.VMEM((EXL * GSLOT, 128), BF),
                pltpu.VMEM((EXL, D, FFL), BF),
                pltpu.VMEM((EXL, D, FFL), BF),
                pltpu.SemaphoreType.DMA((2,)),
            ],
        ),
        compiler_params=pltpu.CompilerParams(vmem_limit_bytes=VMEM_MAX),
        name="experts_up",
    )(base, xg, w_gate, w_up)


def combine_kernel(
    inner_ref, wd_hbm, wdp_hbm, xg_hbm, out_ref,
    inner2, wdh, meta, outc, want, yp, st1, fin1, st2, fin2, fin3, land,
    lsem, isem, s1, r1, s2, r2, s3, r3, esem,
):
    x, z, c, y = coords()

    def dev(xx, zz, cc, yy):
        return (xx * 8 + zz * 2 + cc, yy)

    other = dev(x, z, 1 - c, y)
    greet(
        [dev(wrap(x + 1), z, c, y), dev(wrap(x - 1), z, c, y), dev(x, wrap(z + 1), c, y), dev(x, wrap(z - 1), c, y)]
        + [other]
        + [dev(x, z, c, wrap(y + k)) for k in (1, 2, 3)]
    )
    waits = []

    def ship(src, dst, target, send, recv):
        copy = pltpu.make_async_remote_copy(
            src_ref=src, dst_ref=dst, send_sem=send, recv_sem=recv, device_id=target, device_id_type=MESH
        )
        copy.start()
        waits.append(copy)
        return copy

    def expect(ref, sem):
        pltpu.make_async_copy(ref, ref, sem).wait()

    swap = ship(inner_ref, inner2, other, isem.at[0], isem.at[1])
    near = pl.ds(pl.multiple_of(c * HALF, HALF), HALF)
    loads = [
        pltpu.make_async_copy(wd_hbm.at[:, :, near], wdh.at[c], lsem.at[0]),
        pltpu.make_async_copy(wdp_hbm, wdh.at[1 - c], lsem.at[1]),
        pltpu.make_async_copy(xg_hbm.at[:, :, pl.ds(D, META)], meta, lsem.at[2]),
    ]
    for load in loads:
        load.start()
    want[...] = slot_numbers((GROUP, 2 * EXL * GSLOT), 1)
    lanes = expert_lanes((128, 2 * EXL * GSLOT), 1, (x * 4 + z) * 2 * EXL)

    def down(core, source):
        @pl.loop(0, EXL)
        def _(e):
            row = pl.multiple_of((core * EXL + e) * GSLOT, 16)
            for n in range(2):
                cols = slice(n * BLK, (n + 1) * BLK)
                part = jnp.dot(source[e], wdh[core, e, :, cols], preferred_element_type=F32).astype(BF)
                for q in range(4):
                    outc[n, q, pl.ds(row, GSLOT), :] = part[q * GSLOT : (q + 1) * GSLOT]

    loads[0].wait()
    down(c, inner_ref)
    loads[1].wait()
    swap.wait_recv()
    down(1 - c, inner2)
    loads[2].wait()

    def scatter(col):
        @pl.loop(0, 4)
        def _(q):
            named = jnp.dot(meta[q, :, 0:128], lanes, preferred_element_type=F32)
            gate = jnp.dot(meta[q, :, 128:256], lanes, preferred_element_type=F32)
            mix = jnp.where(named == want[...], gate, 0.0).astype(BF)
            part = jnp.dot(mix, outc[col, q], preferred_element_type=F32).astype(BF)
            for k in range(4):
                piece = part[k * 128 : (k + 1) * 128]
                if col == 0:
                    yp[0, q, k] = piece
                else:
                    yp[1, k, q] = piece

    first, second = (x, z), (z, x)

    def fdev(col, f):
        return dev(f, z, c, y) if col == 0 else dev(x, f, c, y)

    def sdev(col, s):
        return dev(x, s, c, y) if col == 0 else dev(s, z, c, y)

    def open1(col):
        p = first[col]
        up, dn = fdev(col, wrap(p + 1)), fdev(col, wrap(p - 1))
        ship(yp.at[col, wrap(p + 2), pl.ds(0, 2)], st1.at[col, 0], up, s1.at[col, 0], r1.at[col, 0])
        ship(yp.at[col, wrap(p + 2), pl.ds(2, 2)], st1.at[col, 1], dn, s1.at[col, 1], r1.at[col, 1])
        ship(yp.at[col, wrap(p + 1), pl.ds(2, 2)], fin1.at[col, 0, pl.ds(2, 2)], up, s1.at[col, 2], r1.at[col, 2])
        ship(yp.at[col, wrap(p - 1), pl.ds(0, 2)], fin1.at[col, 1, pl.ds(0, 2)], dn, s1.at[col, 3], r1.at[col, 3])

    def mid1(col):
        p = first[col]
        up, dn = fdev(col, wrap(p + 1)), fdev(col, wrap(p - 1))
        for side, (f, lo, target) in enumerate(((wrap(p + 1), 0, up), (wrap(p - 1), 2, dn))):
            expect(st1.at[col, side], r1.at[col, side])
            for k in range(2):
                acc = yp[col, f, lo + k].astype(F32) + st1[col, side, k].astype(F32)
                yp[col, f, lo + k] = acc.astype(BF)
            ship(
                yp.at[col, f, pl.ds(lo, 2)],
                fin1.at[col, side, pl.ds(lo, 2)],
                target,
                s1.at[col, 4 + side],
                r1.at[col, 4 + side],
            )

    def end1(col):
        p, s = first[col], second[col]
        for side, lo in ((0, 2), (1, 0), (0, 0), (1, 2)):
            expect(
                fin1.at[col, side, pl.ds(lo, 2)],
                r1.at[col, {(0, 2): 2, (1, 0): 3, (0, 0): 4, (1, 2): 5}[(side, lo)]],
            )
        up, dn = sdev(col, wrap(s + 1)), sdev(col, wrap(s - 1))

        def fold(t):
            acc = yp[col, p, t].astype(F32) + fin1[col, 0, t].astype(F32) + fin1[col, 1, t].astype(F32)
            yp[col, p, t] = acc.astype(BF)

        lo, hi = pl.ds(0, 64), pl.ds(64, 64)
        t = wrap(s + 2)
        fold(t)
        ship(yp.at[col, p, t, lo], st2.at[col, 0], up, s2.at[col, 0], r2.at[col, 0])
        ship(yp.at[col, p, t, hi], st2.at[col, 1], dn, s2.at[col, 1], r2.at[col, 1])
        t = wrap(s + 1)
        fold(t)
        ship(yp.at[col, p, t, hi], fin2.at[col, 0, hi], up, s2.at[col, 2], r2.at[col, 2])
        t = wrap(s - 1)
        fold(t)
        ship(yp.at[col, p, t, lo], fin2.at[col, 1, lo], dn, s2.at[col, 3], r2.at[col, 3])
        fold(s)

    def mid2(col):
        p, s = first[col], second[col]
        up, dn = sdev(col, wrap(s + 1)), sdev(col, wrap(s - 1))
        for side, (t, lo, target) in enumerate(((wrap(s + 1), 0, up), (wrap(s - 1), 64, dn))):
            expect(st2.at[col, side], r2.at[col, side])
            acc = yp[col, p, t, lo : lo + 64].astype(F32) + st2[col, side].astype(F32)
            yp[col, p, t, lo : lo + 64] = acc.astype(BF)
            rows = pl.ds(lo, 64)
            ship(
                yp.at[col, p, t, rows], fin2.at[col, side, rows], target, s2.at[col, 4 + side], r2.at[col, 4 + side]
            )

    def end2(col):
        p, s = first[col], second[col]
        for side, lo, k in ((0, 64, 2), (1, 0, 3), (0, 0, 4), (1, 64, 5)):
            expect(fin2.at[col, side, pl.ds(lo, 64)], r2.at[col, k])
        acc = yp[col, p, s].astype(F32) + fin2[col, 0].astype(F32) + fin2[col, 1].astype(F32)
        yp[col, p, s] = acc.astype(BF)
        goal = 2 * c + col
        for k in (1, 2, 3):

            @pl.when(wrap(goal + k) == y)
            def _():
                copy = pltpu.make_async_remote_copy(
                    src_ref=yp.at[col, p, s],
                    dst_ref=fin3.at[k - 1],
                    send_sem=s3.at[col],
                    recv_sem=r3.at[k - 1],
                    device_id=dev(x, z, c, goal),
                    device_id_type=MESH,
                )
                copy.start()

    def end3(col):
        p, s = first[col], second[col]

        @pl.when(y == 2 * c + col)
        def _():
            for k in range(3):
                expect(fin3.at[k], r3.at[k])
            acc = yp[col, p, s].astype(F32)
            for k in range(3):
                acc = acc + fin3[k].astype(F32)
            yp[col, p, s] = acc.astype(BF)
            copy = pltpu.make_async_remote_copy(
                src_ref=yp.at[col, p, s, pl.ds(pl.multiple_of((1 - c) * 64, 64), 64)],
                dst_ref=land,
                send_sem=esem.at[0],
                recv_sem=esem.at[1],
                device_id=other,
                device_id_type=MESH,
            )
            copy.start()
            out_ref[...] = yp[col, p, s, pl.ds(pl.multiple_of(c * 64, 64), 64)]
            copy.wait_send()

        @pl.when(y != 2 * c + col)
        def _():
            expect(yp.at[col, p, s], s3.at[col])

    scatter(0)
    open1(0)
    scatter(1)
    open1(1)
    for step in (mid1, end1, mid2, end2, end3):
        for col in (0, 1):
            step(col)

    @pl.when(y // 2 != c)
    def _():
        expect(land, esem.at[1])
        out_ref[...] = land[...]

    for copy in waits:
        copy.wait_send()


def combine(inner, w_down, wd_far, xg):
    return pl.pallas_call(
        combine_kernel,
        out_shape=jax.ShapeDtypeStruct((ROWS, BLK), BF),
        in_specs=[pl.BlockSpec(memory_space=pltpu.VMEM)] + [pl.BlockSpec(memory_space=pl.ANY)] * 3,
        out_specs=pl.BlockSpec(memory_space=pltpu.VMEM),
        scratch_shapes=[
            pltpu.VMEM((EXL, 4 * GSLOT, FFL), BF),
            pltpu.VMEM((2, EXL, FFL, HALF), BF),
            pltpu.VMEM((4, GROUP, META), BF),
            pltpu.VMEM((2, 4, 2 * EXL * GSLOT, BLK), BF),
            pltpu.VMEM((GROUP, 2 * EXL * GSLOT), F32),
            pltpu.VMEM((2, 4, 4, 128, BLK), BF),
            pltpu.VMEM((2, 2, 2, 128, BLK), BF),
            pltpu.VMEM((2, 2, 4, 128, BLK), BF),
            pltpu.VMEM((2, 2, 64, BLK), BF),
            pltpu.VMEM((2, 2, 128, BLK), BF),
            pltpu.VMEM((3, 128, BLK), BF),
            pltpu.VMEM((64, BLK), BF),
            pltpu.SemaphoreType.DMA((3,)),
            pltpu.SemaphoreType.DMA((2,)),
            pltpu.SemaphoreType.DMA((2, 6)),
            pltpu.SemaphoreType.DMA((2, 6)),
            pltpu.SemaphoreType.DMA((2, 6)),
            pltpu.SemaphoreType.DMA((2, 6)),
            pltpu.SemaphoreType.DMA((2,)),
            pltpu.SemaphoreType.DMA((3,)),
            pltpu.SemaphoreType.DMA((2,)),
        ],
        compiler_params=pltpu.CompilerParams(
            collective_id=1, has_side_effects=True, vmem_limit_bytes=VMEM_MAX
        ),
        name="combine",
    )(inner, w_down, wd_far, xg)


def attend_kernel(slot_ref, lens_ref, q_ref, page_ref, far_ref, out_ref):
    r = pl.program_id(0)
    page = jnp.where(r == slot_ref[0], far_ref[...], page_ref[0])
    scores = lax.dot_general(q_ref[0], page, (((1,), (1,)), ((), ())), preferred_element_type=F32)
    scores = scores * SCORE_SCALE
    live = lax.broadcasted_iota(jnp.int32, scores.shape, 1) < lens_ref[r]
    scores = jnp.where(live, scores, MASK_FLOOR)
    weight = jnp.where(live, jnp.exp(scores - jnp.max(scores, axis=1, keepdims=True)), 0.0)
    total = jnp.sum(weight, axis=1, keepdims=True)
    blended = jnp.dot(weight.astype(BF), page[:, :LAT], preferred_element_type=F32)
    out_ref[0] = (blended / total).astype(BF)


def attend(slot, lens, queries, pages, far):
    count, heads, width = queries.shape
    ctx = pages.shape[1]
    return pl.pallas_call(
        attend_kernel,
        out_shape=jax.ShapeDtypeStruct((count, heads, LAT), BF),
        grid_spec=pltpu.PrefetchScalarGridSpec(
            num_scalar_prefetch=2,
            grid=(count,),
            in_specs=[
                pl.BlockSpec((1, heads, width), lambda r, *_: (r, 0, 0)),
                pl.BlockSpec((1, ctx, width), lambda r, *_: (r, 0, 0)),
                pl.BlockSpec((ctx, width), lambda r, *_: (0, 0)),
            ],
            out_specs=pl.BlockSpec((1, heads, LAT), lambda r, *_: (r, 0, 0)),
        ),
        name="attend",
    )(slot, lens, queries, pages, far)


def trade(page, mask):
    count = lax.axis_size("ep")

    def branch(m):
        return lambda block: lax.ppermute(block, "ep", [(i, i ^ m) for i in range(count)])

    return lax.switch(mask - 1, [branch(m) for m in range(1, count)], page)


def local(
    cache_pages,
    queries,
    lengths,
    swap_slot,
    swap_mask,
    hidden,
    expert_ids,
    gate_weights,
    w_gate,
    w_up,
    w_down,
):
    ep_rank = lax.axis_index("ep")
    groups = lax.axis_size("tp")
    tp_rank = lax.axis_index("tp")

    lane = jnp.arange(128, dtype=jnp.int32)
    hits = expert_ids[:, :, None] == lane[None, None, :]
    chosen = jnp.any(hits, axis=1)
    gates = jnp.sum(jnp.where(hits, gate_weights[:, :, None], 0.0), axis=1)
    upto = jnp.arange(ROWS)[:, None] >= jnp.arange(ROWS)[None, :]
    place = jnp.dot(upto.astype(BF), chosen.astype(BF), preferred_element_type=F32)
    table = jnp.where(chosen, place, 0.0)
    xin = jnp.concatenate([hidden, table.astype(BF), gates.astype(BF)], axis=1)
    xg, wd_far = gather_rows(xin, w_down)
    xg = xg.reshape(4, GROUP, XW)
    base = (ep_rank * EXL).astype(jnp.int32).reshape(1)
    inner = experts_up(base, xg, w_gate, w_up)
    moe_rows = combine(inner, w_down, wd_far, xg)

    count = cache_pages.shape[0]
    device = ep_rank * groups + tp_rank
    partner = jnp.bitwise_xor(ep_rank, swap_mask[0]) * groups + tp_rank
    my_slot = swap_slot[device]
    far_slot = swap_slot[partner]
    own_lengths = lax.dynamic_slice_in_dim(lengths, device * count, count)
    live_lengths = jnp.where(
        jnp.arange(count, dtype=jnp.int32) == my_slot, lengths[partner * count + far_slot], own_lengths
    )
    own_page = lax.dynamic_index_in_dim(cache_pages, my_slot, 0, keepdims=False)
    arrived = trade(own_page, swap_mask[0])
    attended = attend(my_slot.reshape(1), live_lengths, queries, cache_pages, arrived)
    return attended, moe_rows


def solution(mesh):
    in_specs = (
        P(("ep", "tp"), None, None),
        P(("ep", "tp"), None, None),
        P(),
        P(),
        P(),
        P("ep", None),
        P("ep", None),
        P("ep", None),
        P("ep", None, "tp"),
        P("ep", None, "tp"),
        P("ep", "tp", None),
    )
    out_specs = (P(("ep", "tp"), None, None), P("ep", "tp"))
    return jax.shard_map(local, mesh=mesh, in_specs=in_specs, out_specs=out_specs, check_vma=False)
```

time: 408 us -> 190 us (0.47)
  blocking collectives: 221 us -> 0 us
  Pallas kernels: 0 us -> 152 us
  local copies, waits for them, and re-layouts: 78.5 us -> 18.9 us
  matrix products: 39.6 us -> 0.13 us
  waiting for transfers between devices: 40.5 us -> 7.1 us
  between operations: 17.5 us -> 3.68 us
    all_to_all x2 -> x0, blocking collectives: 221 us -> none  [the longest x1 113 us: local(): lax.all_to_all(outgoing, 'ep', split_axis=0, concat_axis=0, tiled=True)]
    pallas_call x0 -> x4, Pallas kernels: none -> 152 us  [the longest x1 66.7 us: combine(): pl.pallas_call(combine_kernel, out_shape=jax.ShapeDtypeStruct((ROWS, BLK)...]
    dot_general x5 -> x1, matrix products: 35.1 us -> 0.13 us  [local(): jnp.dot(upto.astype(BF), chosen.astype(BF), preferred_element_type=F32)]
    reshape x3 -> x0, local copies, waits for them, and re-layouts: 32.1 us -> none  [the longest x2 20.8 us: local(): outgoing = outgoing.reshape(ep_size, expert_local, capacity, model_width)]
    ppermute x5 -> x1, waiting for transfers between devices: 25 us -> 7.1 us  [branch(): lax.ppermute(block, 'ep', [(i, i ^ m) for i in range(count)])]
    unnamed x2 -> x0, waiting for transfers between devices: 15.4 us -> none
    all_to_all x1 -> x0, local copies, waits for them, and re-layouts: 10.8 us -> none  [local(): lax.all_to_all(partials, 'ep', split_axis=0, concat_axis=0, tiled=True)]
    convert_element_type x1 -> x0, local copies, waits for them, and re-layouts: 9.11 us -> none  [local(): partials = jnp.einsum('sejf,efd->sejd', inner_act, w_down, preferred_elem...]
  transfers between devices with their start and end apart: 6 -> 1, of which waited for: 5 -> 1; matrix products, arithmetic and copies ran while one was open for 6% -> 0% of each run, Pallas kernels for 0% -> 0%
where the time goes in v1:
time: 190 us; the launch traced here: 189 us
  Pallas kernels  152 us (80%)
  local copies, waits for them, and re-layouts  18.9 us (10%)
  waiting for transfers between devices  7.1 us (4%)
  other arithmetic  4.71 us (2%)
  between operations  3.68 us (2%)
  starting transfers between devices  2.11 us (1%)
    pallas_call x1, Pallas kernels, combine(): pl.pallas_call(combine_kernel, out_shape=jax.ShapeDtypeStruct((ROWS, BLK)...  66.7 us
    pallas_call x1, Pallas kernels, gather_rows(): pl.pallas_call(gather_kernel, out_shape=(jax.ShapeDtypeStruct((4, 4, 2, R...  52 us
    pallas_call x1, Pallas kernels, experts_up(): pl.pallas_call(up_kernel, out_shape=jax.ShapeDtypeStruct((EXL, 4 * GSLOT,...  17.4 us
    pallas_call x1, Pallas kernels, attend(): pl.pallas_call(attend_kernel, out_shape=jax.ShapeDtypeStruct((count, head...  15.8 us
    unnamed x5, local copies, waits for them, and re-layouts  15.2 us
    ppermute x1, waiting for transfers between devices, branch(): lax.ppermute(block, 'ep', [(i, i ^ m) for i in range(count)])  7.1 us
  transfers between devices with their start and end apart: 1, of which 1 were waited for; matrix products, arithmetic and copies ran while one was open for 0% of the time, Pallas kernels for 0%

profile of v1, /device:TPU:1, one launch (start us, length us, event | category | flops | bytes accessed | tf_op | source)
XLA Modules:
  0.0 188.5 jit_solution(2930416272958796342)
XLA Ops:
  1.3 1.3 fusion.2
  5.0 1.3 dynamic_slice.18
  6.2 2.5 %compare_select_fusion.lens_ref = s32[16]{0:T(128)} fusion(s32[2048]{0:T(1024)} %param.44, s32[]{:T(128)S(6)} %select_n.31, s32[]{:T(128)} %bitcast.3, s32[]{:T(128)} %bitcast), kind=kLoop, calls=%fused_computation.7 | loop fusion | flops 32 | bytes 140 | tf_op jit(solution)/shard_map/jit(_where)/select_n | solution.py:624
  8.7 0.8 copy.21
  9.5 0.2 fusion.1
  9.7 0.1 fusion
  9.8 0.8 copy.22
  10.6 0.2 select_reduce_fusion
  10.8 1.0 constant_dynamic-slice_fusion
  11.8 0.2 copy.18
  12.0 9.2 %conditional.1 = (bf16[256,576]{1,0:T(8,128)(2,1)}) conditional(s32[]{:T(128)} %clamp.3, bf16[256,576]{1,0:T(8,128)(2,1)S(1)} %bitcast.27, bf16[256,576]{1,0:T(8,128)(2,1)S(1)} %bitcast.42, bf16[256,576]{1,0:T(8,128)(2,1)S(1)} %bitcast.14, bf16[256,576]{1,0:T(8,128)(2,1)S(1)} %bitcast.15, ...), branch_computations={%region_0.0_spmd, %region_1.2_spmd, %region_2.3_spmd, %region_3.4_... | conditional | bytes 1179696 | solution.py:584
  12.0 2.1 %collective-permute-start.7 = (bf16[256,576]{1,0:T(8,128)(2,1)S(1)}, bf16[256,576]{1,0:T(8,128)(2,1)}, u32[]{:S(2)}, u32[]{:S(2)}) collective-permute-start(bf16[256,576]{1,0:T(8,128)(2,1)S(1)} %param.7), channel_id=1, source_target_pairs={{0,32},{4,36},{8,40},{12,44},{16,48},{20,52},{24,56},{28,60},{32,0... | collective-permute-start | bytes 884744 | tf_op jit(solution)/shard_map/cond/branch_7_fun/ppermute | solution.py:582
  14.1 7.1 %collective-permute-done.7 = bf16[256,576]{1,0:T(8,128)(2,1)} collective-permute-done((bf16[256,576]{1,0:T(8,128)(2,1)S(1)}, bf16[256,576]{1,0:T(8,128)(2,1)}, u32[]{:S(2)}, u32[]{:S(2)}) %collective-permute-start.7) | collective-permute-done | bytes 294944 | tf_op jit(solution)/shard_map/cond/branch_7_fun/ppermute | solution.py:582
  21.2 1.8 pad_maximum_fusion.x_ref
  23.1 4.4 %copy.19.q_ref = bf16[16,128,576]{2,1,0:T(8,128)(2,1)} copy(bf16[16,128,576]{1,2,0:T(8,128)(2,1)} %param.43) | data formatting | bytes 4718592 | tf_op args[1]
  27.4 7.7 %copy.20.page_ref = bf16[16,256,576]{2,1,0:T(8,128)(2,1)} copy(bf16[16,256,576]{1,2,0:T(8,128)(2,1)} %param.42) | data formatting | bytes 9437184 | tf_op args[0]
  35.1 15.8 %attend.1 = bf16[16,128,512]{2,1,0:T(8,128)(2,1)} custom-call(s32[1]{0:T(128)} %get-tuple-element.70.slot_ref, s32[16]{0:T(128)} %compare_select_fusion.lens_ref, bf16[16,128,576]{2,1,0:T(8,128)(2,1)} %copy.19.q_ref, bf16[16,256,576]{2,1,0:T(8,128)(2,1)} %copy.20.page_ref, bf16[256,576]{1,0:T(8,128)(2,1)} %get-tuple-element.75.far_ref), custom_call_target="tpu_custom_call" | custom-call | tf_op jit(solution)/shard_map/attend/pallas_call | solution.py:561
  50.9 52.0 %gather_rows.1 = (bf16[4,4,2,64,3840]{4,3,2,1,0:T(8,128)(2,1)}, bf16[3,256,1792]{2,1,0:T(8,128)(2,1)}) custom-call(bf16[64,3840]{1,0:T(8,128)(2,1)} %pad_maximum_fusion.x_ref, bf16[3,256,3584]{2,1,0:T(8,128)(2,1)} %wd_hbm.1), custom_call_target="tpu_custom_call" | custom-call | tf_op jit(solution)/shard_map/gather_rows/pallas_call | solution.py:194
  103.0 17.4 %experts_up.1.inner_ref = bf16[3,320,256]{2,1,0:T(8,128)(2,1)} custom-call(s32[1]{0:T(128)} %bitcast.5.base_ref, bf16[4,512,3840]{2,1,0:T(8,128)(2,1)} %bitcast.10, bf16[3,3584,256]{2,1,0:T(8,128)(2,1)} %wg_hbm.1, bf16[3,3584,256]{2,1,0:T(8,128)(2,1)} %wu_hbm.1), custom_call_target="tpu_custom_call" | custom-call | tf_op jit(solution)/shard_map/experts_up/pallas_call | solution.py:276
  120.3 66.7 %combine.1 = bf16[64,896]{1,0:T(8,128)(2,1)} custom-call(bf16[3,320,256]{2,1,0:T(8,128)(2,1)} %experts_up.1.inner_ref, bf16[3,256,3584]{2,1,0:T(8,128)(2,1)} %wd_hbm.1, bf16[3,256,1792]{2,1,0:T(8,128)(2,1)} %get-tuple-element.68.wdp_hbm, bf16[4,512,3840]{2,1,0:T(8,128)(2,1)} %bitcast.11), custom_call_target="tpu_custom_call" | custom-call | tf_op jit(solution)/shard_map/combine/pallas_call | solution.py:510
  187.0 1.6 copy.56
Async XLA Ops:
  12.0 9.2 %collective-permute-start.7 = (bf16[256,576]{1,0:T(8,128)(2,1)S(1)}, bf16[256,576]{1,0:T(8,128)(2,1)}, u32[]{:S(2)}, u32[]{:S(2)}) collective-permute-start(bf16[256,576]{1,0:T(8,128)(2,1)S(1)} %param.7), channel_id=1, source_target_pairs={{0,32},{4,36},{8,40},{12,44},{16,48},{20,52},{24,56},{28,60},{32,0... | collective-permute-start | bytes 884744 | tf_op jit(solution)/shard_map/cond/branch_7_fun/ppermute | solution.py:582

commit v2 on v1

v2 whole, which is shorter than its diff:
```python
import functools

import jax
import jax.numpy as jnp
from jax import lax
from jax.experimental import pallas as pl
from jax.experimental.pallas import tpu as pltpu
from jax.sharding import PartitionSpec as P

MESH = pl.DeviceIdType.MESH
BF = jnp.bfloat16
F32 = jnp.float32
LAT = 512
D = 3584
ROWS = 64
CAP = 10
EXL = 3
META = 256
GROUP = 512
GSLOT = 80
HALF = D // 2
BLK = D // 4
FFL = 256
SCORE_SCALE = 192.0 ** (-0.5)
MASK_FLOOR = -1e30
VMEM_MAX = 60 * 1024 * 1024


def coords():
    e = lax.axis_index("ep")
    return e // 8, lax.rem(e // 2, 4), lax.rem(e, 2), lax.axis_index("tp")


def wrap(v):
    return lax.rem(v + 4, 4)


def greet(targets):
    barrier = pltpu.get_barrier_semaphore()
    for target in targets:
        pl.semaphore_signal(barrier, inc=1, device_id=target, device_id_type=MESH)
    pl.semaphore_wait(barrier, len(targets))


QUARTER = 256
MAIN = D - 4 * QUARTER
WHOLE = MAIN + META


def gather_kernel(
    x_ref, xp_ref, wd_ref, xg_ref, xq_ref, wdp_ref,
    ssem, rsem1, rsem2, dsend, drecv, ysend, yrecv, ydsend, ydrecv, wsem, lsem,
):
    x, z, c, y = coords()

    def dev(xx, zz, cc):
        return (xx * 8 + zz * 2 + cc, y)

    other = dev(x, z, 1 - c)
    above, below = (x * 8 + z * 2 + c, wrap(y + 1)), (x * 8 + z * 2 + c, wrap(y - 1))
    started = []
    count = {}

    def push(src, dst, target, send, recv):
        copy = pltpu.make_async_remote_copy(
            src_ref=src, dst_ref=dst, send_sem=send, recv_sem=recv, device_id=target, device_id_type=MESH
        )
        copy.start()
        started.append(copy)

    def ship(part, col, src, dst, target, recv):
        k = count.get((part, col), 0)
        count[part, col] = k + 1
        push(src, dst, target, ssem.at[part, col, k], recv)

    first = (x, z)
    second = (z, x)

    def place(part, col, f, s, lo=0, size=32):
        xx, zz = (f, s) if col == 0 else (s, f)
        rows = pl.ds(col * 32 + lo, size)
        return xg_ref.at[xx, zz, c, rows] if part else xq_ref.at[y, xx, zz, c, rows]

    def line(col, s, yy, lo=0, size=4, core=c):
        rows = pl.ds(col * 32, 32)
        if col == 0:
            return xq_ref.at[yy, pl.ds(lo, size), s, core, rows]
        return xq_ref.at[yy, s, pl.ds(lo, size), core, rows]

    def fdev(col, f):
        return dev(f, z, c) if col == 0 else dev(x, f, c)

    def sdev(col, s):
        return dev(x, s, c) if col == 0 else dev(s, z, c)

    def own(part, col):
        rows = pl.ds(col * 32, 32)
        return x_ref.at[rows] if part else xp_ref.at[y, rows]

    def expect(ref, sem):
        pltpu.make_async_copy(ref, ref, sem).wait()

    def share(part, col, f, s, src=None):
        if part == 0:
            return
        xx, zz = (f, s) if col == 0 else (s, f)
        slot = xx * 4 + zz
        ref = place(part, col, f, s)
        push(ref if src is None else src, ref, other, dsend.at[col, slot], drecv.at[col, slot])

    def fan(part, col, k, f, src=None):
        s = second[col]
        ref = place(part, col, f, s)
        src = ref if src is None else src
        ship(part, col, src, ref, sdev(col, wrap(s + 1)), rsem2.at[part, col, k, 0])
        ship(part, col, src, ref, sdev(col, wrap(s - 1)), rsem2.at[part, col, k, 1])

    def relay2(part, col, k, f):
        s = second[col]
        expect(place(part, col, f, wrap(s - 1)), rsem2.at[part, col, k, 0])
        ref = place(part, col, f, wrap(s - 1), 0, 16)
        ship(part, col, ref, ref, sdev(col, wrap(s + 1)), rsem2.at[part, col, k, 2])
        share(part, col, f, wrap(s - 1))
        expect(place(part, col, f, wrap(s + 1)), rsem2.at[part, col, k, 1])
        ref = place(part, col, f, wrap(s + 1), 16, 16)
        ship(part, col, ref, ref, sdev(col, wrap(s - 1)), rsem2.at[part, col, k, 3])
        share(part, col, f, wrap(s + 1))

    def last2(part, col, k, f):
        s = wrap(second[col] + 2)
        expect(place(part, col, f, s, 0, 16), rsem2.at[part, col, k, 2])
        expect(place(part, col, f, s, 16, 16), rsem2.at[part, col, k, 3])
        share(part, col, f, s)

    def open1(part):
        for col in (0, 1):
            p, s = first[col], second[col]
            ref = place(part, col, p, s)
            ship(part, col, own(part, col), ref, fdev(col, wrap(p + 1)), rsem1.at[part, col, 0])
            ship(part, col, own(part, col), ref, fdev(col, wrap(p - 1)), rsem1.at[part, col, 1])

    def relay1(part):
        for col in (0, 1):
            p, s = first[col], second[col]
            expect(place(part, col, wrap(p - 1), s), rsem1.at[part, col, 0])
            ref = place(part, col, wrap(p - 1), s, 0, 16)
            ship(part, col, ref, ref, fdev(col, wrap(p + 1)), rsem1.at[part, col, 2])
            expect(place(part, col, wrap(p + 1), s), rsem1.at[part, col, 1])
            ref = place(part, col, wrap(p + 1), s, 16, 16)
            ship(part, col, ref, ref, fdev(col, wrap(p - 1)), rsem1.at[part, col, 3])
            if part:
                for k, f in ((1, wrap(p - 1)), (2, wrap(p + 1))):
                    fan(1, col, k, f)
                    share(1, col, f, s)

    def last1(part, col):
        p, s = first[col], second[col]
        expect(place(part, col, wrap(p + 2), s, 0, 16), rsem1.at[part, col, 2])
        expect(place(part, col, wrap(p + 2), s, 16, 16), rsem1.at[part, col, 3])

    def source(col, k):
        return wrap(first[col] + (0, -1, 1, 2)[k])

    def lines_out(col):
        s = second[col]
        ref = line(col, s, y)
        ship(0, col, ref, ref, sdev(col, wrap(s + 1)), rsem2.at[0, col, 0, 0])
        ship(0, col, ref, ref, sdev(col, wrap(s - 1)), rsem2.at[0, col, 0, 1])

    def lines_on(col):
        s = second[col]
        expect(line(col, wrap(s - 1), y), rsem2.at[0, col, 0, 0])
        ref = line(col, wrap(s - 1), y, 0, 2)
        ship(0, col, ref, ref, sdev(col, wrap(s + 1)), rsem2.at[0, col, 0, 2])
        expect(line(col, wrap(s + 1), y), rsem2.at[0, col, 0, 1])
        ref = line(col, wrap(s + 1), y, 2, 2)
        ship(0, col, ref, ref, sdev(col, wrap(s - 1)), rsem2.at[0, col, 0, 3])

    def lines_in(col):
        s = wrap(second[col] + 2)
        expect(line(col, s, y, 0, 2), rsem2.at[0, col, 0, 2])
        expect(line(col, s, y, 2, 2), rsem2.at[0, col, 0, 3])

    def part_of(yy, lo, size=2, core=c):
        return xq_ref.at[yy, pl.ds(lo, size), :, core]

    def hand(d):
        ref = part_of(wrap(y + d), 0, 4)
        push(ref, ref, other, ydsend.at[d], ydrecv.at[d])

    locals_ = [
        pltpu.make_async_copy(xp_ref.at[y], xq_ref.at[y, x, z, c], lsem.at[0]),
        pltpu.make_async_copy(x_ref, xg_ref.at[x, z, c], lsem.at[1]),
    ]
    for copy in locals_:
        copy.start()
    greet(
        [dev(wrap(x + 1), z, c), dev(wrap(x - 1), z, c), dev(x, wrap(z + 1), c), dev(x, wrap(z - 1), c)]
        + [other, above, below]
    )
    open1(0)
    open1(1)
    far = pl.ds(pl.multiple_of((1 - c) * HALF, HALF), HALF)
    push(wd_ref.at[:, :, far], wdp_ref, other, wsem.at[0], wsem.at[1])
    relay1(0)
    locals_[0].wait()
    for col in (0, 1):
        last1(0, col)
        lines_out(col)
    for col in (0, 1):
        lines_on(col)
    for col in (0, 1):
        fan(1, col, 0, first[col], own(1, col))
        share(1, col, first[col], second[col], own(1, col))
    relay1(1)
    for col in (0, 1):
        lines_in(col)
    for k, lo, target in ((0, 0, above), (2, 2, below), (1, 2, above), (3, 0, below)):
        ref = part_of(y, lo)
        push(ref, ref, target, ysend.at[k], yrecv.at[k])
    hand(0)
    for col in (0, 1):
        relay2(1, col, 0, source(col, 0))
    for col in (0, 1):
        last1(1, col)
        fan(1, col, 3, source(col, 3))
        share(1, col, source(col, 3), second[col])
    ref = part_of(wrap(y - 1), 0)
    expect(ref, yrecv.at[0])
    push(ref, ref, above, ysend.at[4], yrecv.at[4])
    ref = part_of(wrap(y + 1), 2)
    expect(ref, yrecv.at[2])
    push(ref, ref, below, ysend.at[5], yrecv.at[5])
    for k in (1, 2):
        for col in (0, 1):
            relay2(1, col, k, source(col, k))
    for col in (0, 1):
        last2(1, col, 0, source(col, 0))
    expect(part_of(wrap(y - 1), 2), yrecv.at[1])
    hand(3)
    expect(part_of(wrap(y + 1), 0), yrecv.at[3])
    hand(1)
    for col in (0, 1):
        relay2(1, col, 3, source(col, 3))
    expect(part_of(wrap(y + 2), 0), yrecv.at[4])
    expect(part_of(wrap(y + 2), 2), yrecv.at[5])
    hand(2)
    for k in (1, 2, 3):
        for col in (0, 1):
            last2(1, col, k, source(col, k))
    for col in (0, 1):
        for slot in range(16):
            expect(xg_ref.at[slot // 4, slot % 4, 1 - c, pl.ds(col * 32, 32)], drecv.at[col, slot])
    for d in range(4):
        expect(part_of(wrap(y + d), 0, 4, 1 - c), ydrecv.at[d])
    expect(wdp_ref, wsem.at[1])
    locals_[1].wait()
    for copy in started:
        copy.wait_send()


def gather_rows(xmain, xparts, w_down):
    dma = pltpu.SemaphoreType.DMA
    return pl.pallas_call(
        gather_kernel,
        out_shape=(
            jax.ShapeDtypeStruct((4, 4, 2, ROWS, WHOLE), BF),
            jax.ShapeDtypeStruct((4, 4, 4, 2, ROWS, QUARTER), BF),
            jax.ShapeDtypeStruct((EXL, FFL, HALF), BF),
        ),
        in_specs=[pl.BlockSpec(memory_space=pltpu.VMEM)] * 2 + [pl.BlockSpec(memory_space=pl.ANY)],
        out_specs=(pl.BlockSpec(memory_space=pl.ANY),) * 3,
        scratch_shapes=[
            dma((2, 2, 20)),
            dma((2, 2, 4)),
            dma((2, 2, 4, 4)),
            dma((2, 16)),
            dma((2, 16)),
            dma((6,)),
            dma((6,)),
            dma((4,)),
            dma((4,)),
            dma((2,)),
            dma((2,)),
        ],
        compiler_params=pltpu.CompilerParams(
            collective_id=0, has_side_effects=True, vmem_limit_bytes=VMEM_MAX
        ),
        name="gather_rows",
    )(xmain, xparts, w_down)


def slot_numbers(shape, axis):
    s = lax.broadcasted_iota(jnp.int32, shape, axis)
    g = lax.broadcasted_iota(jnp.int32, shape, 1 - axis)
    expert = jnp.zeros(shape, jnp.int32)
    for k in range(1, shape[axis] // GSLOT):
        expert = expert + (s >= k * GSLOT).astype(jnp.int32)
    u = s - expert * GSLOT
    rank = (u * 205) >> 11
    want = jnp.where((g >> 6) == rank, u - rank * CAP + 1, -1)
    return want.astype(F32)


def expert_lanes(shape, axis, base):
    s = lax.broadcasted_iota(jnp.int32, shape, axis)
    e = lax.broadcasted_iota(jnp.int32, shape, 1 - axis)
    expert = jnp.zeros(shape, jnp.int32)
    for k in range(1, shape[axis] // GSLOT):
        expert = expert + (s >= k * GSLOT).astype(jnp.int32)
    return jnp.where(expert + base == e, 1.0, 0.0).astype(BF)


def up_kernel(base_ref, x_ref, xp_ref, wg_hbm, wu_hbm, out_ref, xc, want, lanes, wg, wu, sem):
    q = pl.program_id(0)
    gate_copy = pltpu.make_async_copy(wg_hbm, wg, sem.at[0])
    up_copy = pltpu.make_async_copy(wu_hbm, wu, sem.at[1])

    @pl.when(q == 0)
    def _():
        gate_copy.start()
        up_copy.start()
        want[...] = slot_numbers((EXL * GSLOT, GROUP), 0)
        lanes[...] = expert_lanes((EXL * GSLOT, 128), 0, base_ref[0])

    table = x_ref[0, :, MAIN : MAIN + 128]
    named = lax.dot_general(lanes[...], table, (((1,), (1,)), ((), ())), preferred_element_type=F32)
    pick = jnp.where(named == want[...], 1.0, 0.0).astype(BF)
    start = pl.multiple_of(q * GSLOT, 16)

    def keep(rows, cols):
        for e in range(EXL):
            xc[e, pl.ds(start, GSLOT), cols] = rows[e * GSLOT : (e + 1) * GSLOT].astype(BF)

    @pl.loop(0, MAIN // 512)
    def _(n):
        cols = pl.ds(pl.multiple_of(n * 512, 512), 512)
        keep(jnp.dot(pick, x_ref[0, :, cols], preferred_element_type=F32), cols)

    @pl.loop(0, 4)
    def _(n):
        cols = pl.ds(pl.multiple_of(MAIN + n * QUARTER, 128), QUARTER)
        keep(jnp.dot(pick, xp_ref[n, 0], preferred_element_type=F32), cols)

    @pl.when(q == 3)
    def _():
        gate_copy.wait()
        up_copy.wait()

        @pl.loop(0, EXL)
        def _(e):
            gate = jnp.dot(xc[e], wg[e], preferred_element_type=F32)
            up = jnp.dot(xc[e], wu[e], preferred_element_type=F32)
            out_ref[e] = (gate / (1.0 + jnp.exp(-gate)) * up).astype(BF)


def experts_up(base, xg, xq, w_gate, w_up):
    return pl.pallas_call(
        up_kernel,
        out_shape=jax.ShapeDtypeStruct((EXL, 4 * GSLOT, FFL), BF),
        grid_spec=pltpu.PrefetchScalarGridSpec(
            num_scalar_prefetch=1,
            grid=(4,),
            in_specs=[
                pl.BlockSpec((1, GROUP, WHOLE), lambda q, b: (q, 0, 0)),
                pl.BlockSpec((4, 1, GROUP, QUARTER), lambda q, b: (0, q, 0, 0)),
                pl.BlockSpec(memory_space=pl.ANY),
                pl.BlockSpec(memory_space=pl.ANY),
            ],
            out_specs=pl.BlockSpec((EXL, 4 * GSLOT, FFL), lambda q, b: (0, 0, 0)),
            scratch_shapes=[
                pltpu.VMEM((EXL, 4 * GSLOT, D), BF),
                pltpu.VMEM((EXL * GSLOT, GROUP), F32),
                pltpu.VMEM((EXL * GSLOT, 128), BF),
                pltpu.VMEM((EXL, D, FFL), BF),
                pltpu.VMEM((EXL, D, FFL), BF),
                pltpu.SemaphoreType.DMA((2,)),
            ],
        ),
        cost_estimate=pl.CostEstimate(flops=7_000_000_000, bytes_accessed=30_000_000, transcendentals=0),
        compiler_params=pltpu.CompilerParams(vmem_limit_bytes=VMEM_MAX),
        name="experts_up",
    )(base, xg, xq, w_gate, w_up)


def combine_kernel(
    inner_ref, wd_hbm, wdp_hbm, xg_hbm, out_ref,
    inner2, wdh, meta, outc, want, yp, st1, fin1, st2, fin2, fin3,
    lsem, isem, s1, r1, s2, r2, s3, r3,
):
    x, z, c, y = coords()

    def dev(xx, zz, cc, yy):
        return (xx * 8 + zz * 2 + cc, yy)

    other = dev(x, z, 1 - c, y)
    waits = []

    def ship(src, dst, target, send, recv):
        copy = pltpu.make_async_remote_copy(
            src_ref=src, dst_ref=dst, send_sem=send, recv_sem=recv, device_id=target, device_id_type=MESH
        )
        copy.start()
        waits.append(copy)
        return copy

    def expect(ref, sem):
        pltpu.make_async_copy(ref, ref, sem).wait()

    near = pl.ds(pl.multiple_of(c * HALF, HALF), HALF)
    loads = [
        pltpu.make_async_copy(wd_hbm.at[:, :, near], wdh.at[c], lsem.at[0]),
        pltpu.make_async_copy(wdp_hbm, wdh.at[1 - c], lsem.at[1]),
        pltpu.make_async_copy(xg_hbm.at[:, :, pl.ds(MAIN, META)], meta, lsem.at[2]),
    ]
    for load in loads:
        load.start()
    want[...] = slot_numbers((GROUP, 2 * EXL * GSLOT), 1)
    lanes = expert_lanes((128, 2 * EXL * GSLOT), 1, (x * 4 + z) * 2 * EXL)
    greet(
        [dev(wrap(x + 1), z, c, y), dev(wrap(x - 1), z, c, y), dev(x, wrap(z + 1), c, y), dev(x, wrap(z - 1), c, y)]
        + [other]
        + [dev(x, z, core, wrap(y + k)) for k in (1, 2, 3) for core in (0, 1)]
    )
    swap = ship(inner_ref, inner2, other, isem.at[0], isem.at[1])

    def down(core, source):
        @pl.loop(0, EXL)
        def _(e):
            row = pl.multiple_of((core * EXL + e) * GSLOT, 16)
            for n in range(2):
                cols = slice(n * BLK, (n + 1) * BLK)
                part = jnp.dot(source[e], wdh[core, e, :, cols], preferred_element_type=F32).astype(BF)
                for q in range(4):
                    outc[n, q, pl.ds(row, GSLOT), :] = part[q * GSLOT : (q + 1) * GSLOT]

    loads[0].wait()
    down(c, inner_ref)
    loads[1].wait()
    swap.wait_recv()
    down(1 - c, inner2)
    loads[2].wait()

    def scatter(col):
        @pl.loop(0, 4)
        def _(q):
            named = jnp.dot(meta[q, :, 0:128], lanes, preferred_element_type=F32)
            gate = jnp.dot(meta[q, :, 128:256], lanes, preferred_element_type=F32)
            mix = jnp.where(named == want[...], gate, 0.0).astype(BF)
            part = jnp.dot(mix, outc[col, q], preferred_element_type=F32).astype(BF)
            for k in range(4):
                piece = part[k * 128 : (k + 1) * 128]
                if col == 0:
                    yp[0, q, k] = piece
                else:
                    yp[1, k, q] = piece

    first, second = (x, z), (z, x)

    def fdev(col, f):
        return dev(f, z, c, y) if col == 0 else dev(x, f, c, y)

    def sdev(col, s):
        return dev(x, s, c, y) if col == 0 else dev(s, z, c, y)

    def open1(col):
        p = first[col]
        up, dn = fdev(col, wrap(p + 1)), fdev(col, wrap(p - 1))
        ship(yp.at[col, wrap(p + 2), pl.ds(0, 2)], st1.at[col, 0], up, s1.at[col, 0], r1.at[col, 0])
        ship(yp.at[col, wrap(p + 2), pl.ds(2, 2)], st1.at[col, 1], dn, s1.at[col, 1], r1.at[col, 1])
        ship(yp.at[col, wrap(p + 1), pl.ds(2, 2)], fin1.at[col, 0, pl.ds(2, 2)], up, s1.at[col, 2], r1.at[col, 2])
        ship(yp.at[col, wrap(p - 1), pl.ds(0, 2)], fin1.at[col, 1, pl.ds(0, 2)], dn, s1.at[col, 3], r1.at[col, 3])

    def mid1(col):
        p = first[col]
        up, dn = fdev(col, wrap(p + 1)), fdev(col, wrap(p - 1))
        for side, (f, lo, target) in enumerate(((wrap(p + 1), 0, up), (wrap(p - 1), 2, dn))):
            expect(st1.at[col, side], r1.at[col, side])
            for k in range(2):
                acc = yp[col, f, lo + k].astype(F32) + st1[col, side, k].astype(F32)
                yp[col, f, lo + k] = acc.astype(BF)
            ship(
                yp.at[col, f, pl.ds(lo, 2)],
                fin1.at[col, side, pl.ds(lo, 2)],
                target,
                s1.at[col, 4 + side],
                r1.at[col, 4 + side],
            )

    def end1(col):
        p, s = first[col], second[col]
        for side, lo in ((0, 2), (1, 0), (0, 0), (1, 2)):
            expect(
                fin1.at[col, side, pl.ds(lo, 2)],
                r1.at[col, {(0, 2): 2, (1, 0): 3, (0, 0): 4, (1, 2): 5}[(side, lo)]],
            )
        up, dn = sdev(col, wrap(s + 1)), sdev(col, wrap(s - 1))

        def fold(t):
            acc = yp[col, p, t].astype(F32) + fin1[col, 0, t].astype(F32) + fin1[col, 1, t].astype(F32)
            yp[col, p, t] = acc.astype(BF)

        lo, hi = pl.ds(0, 64), pl.ds(64, 64)
        t = wrap(s + 2)
        fold(t)
        ship(yp.at[col, p, t, lo], st2.at[col, 0], up, s2.at[col, 0], r2.at[col, 0])
        ship(yp.at[col, p, t, hi], st2.at[col, 1], dn, s2.at[col, 1], r2.at[col, 1])
        t = wrap(s + 1)
        fold(t)
        ship(yp.at[col, p, t, hi], fin2.at[col, 0, hi], up, s2.at[col, 2], r2.at[col, 2])
        t = wrap(s - 1)
        fold(t)
        ship(yp.at[col, p, t, lo], fin2.at[col, 1, lo], dn, s2.at[col, 3], r2.at[col, 3])
        fold(s)

    def mid2(col):
        p, s = first[col], second[col]
        up, dn = sdev(col, wrap(s + 1)), sdev(col, wrap(s - 1))
        for side, (t, lo, target) in enumerate(((wrap(s + 1), 0, up), (wrap(s - 1), 64, dn))):
            expect(st2.at[col, side], r2.at[col, side])
            acc = yp[col, p, t, lo : lo + 64].astype(F32) + st2[col, side].astype(F32)
            yp[col, p, t, lo : lo + 64] = acc.astype(BF)
            rows = pl.ds(lo, 64)
            ship(
                yp.at[col, p, t, rows], fin2.at[col, side, rows], target, s2.at[col, 4 + side], r2.at[col, 4 + side]
            )

    def end2(col):
        p, s = first[col], second[col]
        for side, lo, k in ((0, 64, 2), (1, 0, 3), (0, 0, 4), (1, 64, 5)):
            expect(fin2.at[col, side, pl.ds(lo, 64)], r2.at[col, k])
        acc = yp[col, p, s].astype(F32) + fin2[col, 0].astype(F32) + fin2[col, 1].astype(F32)
        yp[col, p, s] = acc.astype(BF)
        goal = 2 * c + col

        def final(core, target, k):
            pltpu.make_async_remote_copy(
                src_ref=yp.at[col, p, s, pl.ds(pl.multiple_of(core * 64, 64), 64)],
                dst_ref=fin3.at[k],
                send_sem=s3.at[col, core],
                recv_sem=r3.at[k],
                device_id=target,
                device_id_type=MESH,
            ).start()

        @pl.when(y == goal)
        def _():
            final(1 - c, other, 0)

        for k in (1, 2, 3):

            @pl.when(wrap(goal + k) == y)
            def _():
                for core in (0, 1):
                    final(core, dev(x, z, core, goal), k)

    def end3(col):
        p, s = first[col], second[col]
        half = yp.at[col, p, s, pl.ds(0, 64)]
        expect(half, s3.at[col, 1 - c])

        @pl.when(y != 2 * c + col)
        def _():
            expect(half, s3.at[col, c])

        @pl.when(y == 2 * c + col)
        def _():
            acc = yp[col, p, s, pl.ds(pl.multiple_of(c * 64, 64), 64)].astype(F32)
            for k in (1, 2, 3):
                acc = acc + fin3[k].astype(F32)
            out_ref[...] = acc.astype(BF)

    scatter(0)
    open1(0)
    scatter(1)
    open1(1)
    for step in (mid1, end1, mid2, end2):
        for col in (0, 1):
            step(col)
    for k in (1, 2, 3):
        expect(fin3.at[k], r3.at[k])
    end3(0)
    end3(1)

    @pl.when(y // 2 != c)
    def _():
        expect(fin3.at[0], r3.at[0])
        acc = fin3[0].astype(F32)
        for k in (1, 2, 3):
            acc = acc + fin3[k].astype(F32)
        out_ref[...] = acc.astype(BF)

    for copy in waits:
        copy.wait_send()


def combine(inner, w_down, wd_far, xg):
    return pl.pallas_call(
        combine_kernel,
        out_shape=jax.ShapeDtypeStruct((ROWS, BLK), BF),
        in_specs=[pl.BlockSpec(memory_space=pltpu.VMEM)] + [pl.BlockSpec(memory_space=pl.ANY)] * 3,
        out_specs=pl.BlockSpec(memory_space=pltpu.VMEM),
        scratch_shapes=[
            pltpu.VMEM((EXL, 4 * GSLOT, FFL), BF),
            pltpu.VMEM((2, EXL, FFL, HALF), BF),
            pltpu.VMEM((4, GROUP, META), BF),
            pltpu.VMEM((2, 4, 2 * EXL * GSLOT, BLK), BF),
            pltpu.VMEM((GROUP, 2 * EXL * GSLOT), F32),
            pltpu.VMEM((2, 4, 4, 128, BLK), BF),
            pltpu.VMEM((2, 2, 2, 128, BLK), BF),
            pltpu.VMEM((2, 2, 4, 128, BLK), BF),
            pltpu.VMEM((2, 2, 64, BLK), BF),
            pltpu.VMEM((2, 2, 128, BLK), BF),
            pltpu.VMEM((4, 64, BLK), BF),
            pltpu.SemaphoreType.DMA((3,)),
            pltpu.SemaphoreType.DMA((2,)),
            pltpu.SemaphoreType.DMA((2, 6)),
            pltpu.SemaphoreType.DMA((2, 6)),
            pltpu.SemaphoreType.DMA((2, 6)),
            pltpu.SemaphoreType.DMA((2, 6)),
            pltpu.SemaphoreType.DMA((2, 2)),
            pltpu.SemaphoreType.DMA((4,)),
        ],
        compiler_params=pltpu.CompilerParams(
            collective_id=1, has_side_effects=True, vmem_limit_bytes=VMEM_MAX
        ),
        name="combine",
    )(inner, w_down, wd_far, xg)


def attend_page(query, page, length):
    scores = lax.dot_general(query, page, (((0,), (0,)), ((), ())), preferred_element_type=F32)
    scores = scores * SCORE_SCALE
    live = lax.broadcasted_iota(jnp.int32, scores.shape, 1) < length
    scores = jnp.where(live, scores, MASK_FLOOR)
    weight = jnp.where(live, jnp.exp(scores - jnp.max(scores, axis=1, keepdims=True)), 0.0)
    total = jnp.sum(weight, axis=1, keepdims=True)
    blended = lax.dot_general(
        weight.astype(BF), page[:LAT], (((1,), (1,)), ((), ())), preferred_element_type=F32
    )
    return (blended / total).astype(BF)


def attend_kernel(dev_ref, lens_ref, q_ref, page_ref, out_ref):
    count = q_ref.shape[0]
    base = dev_ref[0] * 16 + pl.program_id(0) * count
    for k in range(count):
        out_ref[k] = attend_page(q_ref[k], page_ref[k], lens_ref[base + k])


def attend(dev, lens, queries, pages):
    count, width, heads = queries.shape
    ctx = pages.shape[2]
    step = 4
    return pl.pallas_call(
        attend_kernel,
        out_shape=jax.ShapeDtypeStruct((count, heads, LAT), BF),
        grid_spec=pltpu.PrefetchScalarGridSpec(
            num_scalar_prefetch=2,
            grid=(count // step,),
            in_specs=[
                pl.BlockSpec((step, width, heads), lambda r, *_: (r, 0, 0)),
                pl.BlockSpec((step, width, ctx), lambda r, *_: (r, 0, 0)),
            ],
            out_specs=pl.BlockSpec((step, heads, LAT), lambda r, *_: (r, 0, 0)),
        ),
        cost_estimate=pl.CostEstimate(flops=2_400_000_000, bytes_accessed=20_000_000, transcendentals=0),
        name="attend",
    )(dev, lens, queries, pages)


def attend_one_kernel(dev_ref, slot_ref, mask_ref, lens_ref, q_ref, page_ref, all_ref, out_ref):
    partner = jnp.bitwise_xor(dev_ref[0], mask_ref[0] * 4)
    length = lens_ref[partner * 16 + slot_ref[partner]]
    out_ref[0] = attend_page(q_ref[0], page_ref[...], length)


def attend_one(dev, slots, mask, lens, queries, page, attended):
    count, width, heads = queries.shape
    return pl.pallas_call(
        attend_one_kernel,
        out_shape=jax.ShapeDtypeStruct(attended.shape, BF),
        grid_spec=pltpu.PrefetchScalarGridSpec(
            num_scalar_prefetch=4,
            grid=(1,),
            in_specs=[
                pl.BlockSpec((1, width, heads), lambda r, dev, slot, *_: (slot[dev[0]], 0, 0)),
                pl.BlockSpec(page.shape, lambda r, *_: (0, 0)),
                pl.BlockSpec(memory_space=pl.ANY),
            ],
            out_specs=pl.BlockSpec((1, heads, LAT), lambda r, dev, slot, *_: (slot[dev[0]], 0, 0)),
        ),
        input_output_aliases={6: 0},
        name="attend_one",
    )(dev, slots, mask, lens, queries, page, attended)


def trade(page, bits, shift, steps, beside):
    count = lax.axis_size("ep")

    def branch(m):
        def run(block):
            if m:
                block = lax.ppermute(block, "ep", [(i, i ^ (m << shift)) for i in range(count)])
            return block, beside()

        return run

    return lax.switch(bits, [branch(m) for m in range(steps)], page)


def prepare_kernel(dev_ref, slot_ref, x_ref, ids_ref, gates_ref, page_ref, out_ref, parts_ref, own_ref):
    own_ref[...] = page_ref[0]
    top = ids_ref.shape[0]
    expert = lax.broadcasted_iota(jnp.int32, (128, ROWS), 0)
    chosen = jnp.zeros((128, ROWS), F32)
    gates = jnp.zeros((128, ROWS), F32)
    for k in range(top):
        hit = expert == ids_ref[k : k + 1, :]
        chosen = jnp.where(hit, 1.0, chosen)
        gates = jnp.where(hit, gates_ref[k : k + 1, :], gates)
    row = lax.broadcasted_iota(jnp.int32, (ROWS, ROWS), 0)
    col = lax.broadcasted_iota(jnp.int32, (ROWS, ROWS), 1)
    upto = jnp.where(row >= col, 1.0, 0.0).astype(BF)
    same = jnp.where(row == col, 1.0, 0.0).astype(BF)
    flip = functools.partial(
        lax.dot_general, dimension_numbers=(((1,), (1,)), ((), ())), preferred_element_type=F32
    )
    chosen = chosen.astype(BF)
    place = jnp.where(flip(same, chosen) > 0.5, flip(upto, chosen), 0.0)
    out_ref[:, :MAIN] = x_ref[:, :MAIN]
    out_ref[:, MAIN : MAIN + 128] = place.astype(BF)
    out_ref[:, MAIN + 128 :] = flip(same, gates.astype(BF)).astype(BF)
    for k in range(4):
        parts_ref[k] = x_ref[:, MAIN + k * QUARTER : MAIN + (k + 1) * QUARTER]


def prepare(dev, slots, hidden, ids, gates, pages):
    count, width, ctx = pages.shape

    def whole(array):
        return pl.BlockSpec(array.shape, lambda r, *_: (0, 0))

    return pl.pallas_call(
        prepare_kernel,
        out_shape=(
            jax.ShapeDtypeStruct((ROWS, WHOLE), BF),
            jax.ShapeDtypeStruct((4, ROWS, QUARTER), BF),
            jax.ShapeDtypeStruct((width, ctx), BF),
        ),
        grid_spec=pltpu.PrefetchScalarGridSpec(
            num_scalar_prefetch=2,
            grid=(1,),
            in_specs=[
                whole(hidden),
                whole(ids),
                whole(gates),
                pl.BlockSpec((1, width, ctx), lambda r, dev, slot: (slot[dev[0]], 0, 0)),
            ],
            out_specs=(
                pl.BlockSpec((ROWS, WHOLE), lambda r, *_: (0, 0)),
                pl.BlockSpec((4, ROWS, QUARTER), lambda r, *_: (0, 0, 0)),
                pl.BlockSpec((width, ctx), lambda r, *_: (0, 0)),
            ),
        ),
        name="prepare",
    )(dev, slots, hidden, ids, gates, pages)


def local(
    cache_pages,
    queries,
    lengths,
    swap_slot,
    swap_mask,
    hidden,
    expert_ids,
    gate_weights,
    w_gate,
    w_up,
    w_down,
):
    ep_rank = lax.axis_index("ep").astype(jnp.int32)
    groups = lax.axis_size("tp")
    tp_rank = lax.axis_index("tp").astype(jnp.int32)
    device = ep_rank * groups + tp_rank
    mask = swap_mask[0]
    dev = device.reshape(1)
    pages = jnp.swapaxes(cache_pages, 1, 2)
    asked = jnp.swapaxes(queries, 1, 2)
    xmain, xparts, own_page = prepare(dev, swap_slot, hidden, expert_ids.T, gate_weights.T, pages)
    page, attended = trade(
        own_page, jnp.right_shift(mask, 3), 3, 4, lambda: attend(dev, lengths, asked, pages)
    )
    xg, xq, wd_far = gather_rows(xmain, xparts, w_down)
    xg = xg.reshape(4, GROUP, WHOLE)
    xq = xq.reshape(4, 4, GROUP, QUARTER)
    base = (ep_rank * EXL).reshape(1)
    page, inner = trade(
        page, jnp.bitwise_and(mask, 7), 0, 8, lambda: experts_up(base, xg, xq, w_gate, w_up)
    )
    moe_rows = combine(inner, w_down, wd_far, xg)
    attended = attend_one(dev, swap_slot, swap_mask, lengths, asked, page, attended)
    return attended, moe_rows


def solution(mesh):
    in_specs = (
        P(("ep", "tp"), None, None),
        P(("ep", "tp"), None, None),
        P(),
        P(),
        P(),
        P("ep", None),
        P("ep", None),
        P("ep", None),
        P("ep", None, "tp"),
        P("ep", None, "tp"),
        P("ep", "tp", None),
    )
    out_specs = (P(("ep", "tp"), None, None), P("ep", "tp"))
    return jax.shard_map(local, mesh=mesh, in_specs=in_specs, out_specs=out_specs, check_vma=False)
```

time: 190 us -> 147 us (0.77)
  local copies, waits for them, and re-layouts: 18.9 us -> 0.68 us
  Pallas kernels: 152 us -> 142 us
  waiting for transfers between devices: 7.1 us -> 0.01 us
  other arithmetic: 4.71 us -> 0 us
  between operations: 3.68 us -> 1.5 us
    unnamed x5 -> x7, local copies, waits for them, and re-layouts: 15.2 us -> 0.66 us
    pallas_call x1, Pallas kernels: 15.8 us -> 7.99 us  [attend(): pl.pallas_call(attend_kernel, out_shape=jax.ShapeDtypeStruct((count, head...]
    ppermute x1, waiting for transfers between devices: 7.1 us -> 0.01 us  [run(): lax.ppermute(block, 'ep', [(i, i ^ m << shift) for i in range(count)])]
    pallas_call x1, Pallas kernels: 66.7 us -> 61.8 us  [combine(): pl.pallas_call(combine_kernel, out_shape=jax.ShapeDtypeStruct((ROWS, BLK)...]
    pallas_call x0 -> x2, Pallas kernels: none -> 4.81 us  [the longest x1 2.8 us: prepare(): pl.pallas_call(prepare_kernel, out_shape=(jax.ShapeDtypeStruct((ROWS, WHO...]
    dynamic_slice x4 -> x0, local copies, waits for them, and re-layouts: 3.79 us -> none  [the longest x1 1.32 us: local(): far_slot = swap_slot[partner]]
    select_n x1 -> x0, other arithmetic: 2.49 us -> none  [local(): jnp.where(jnp.arange(count, dtype=jnp.int32) == my_slot, lengths[partner...]
    pallas_call x1, Pallas kernels: 52 us -> 49.9 us  [gather_rows(): pl.pallas_call(gather_kernel, out_shape=(jax.ShapeDtypeStruct((4, 4, 2, R...]
  transfers between devices with their start and end apart: 1 -> 1, of which waited for: 1 -> 0; matrix products, arithmetic and copies ran while one was open for 0% -> 0% of each run, Pallas kernels for 0% -> 5%
where the time goes in v2:
time: 147 us; the launch traced here: 146 us
  Pallas kernels  142 us (97%)
  starting transfers between devices  2.11 us (1%)
  between operations  1.5 us (1%)
    pallas_call x1, Pallas kernels, combine(): pl.pallas_call(combine_kernel, out_shape=jax.ShapeDtypeStruct((ROWS, BLK)...  61.8 us
    pallas_call x1, Pallas kernels, gather_rows(): pl.pallas_call(gather_kernel, out_shape=(jax.ShapeDtypeStruct((4, 4, 2, R...  49.9 us
    pallas_call x1, Pallas kernels, experts_up(): pl.pallas_call(up_kernel, out_shape=jax.ShapeDtypeStruct((EXL, 4 * GSLOT,...  17.3 us
    pallas_call x1, Pallas kernels, attend(): pl.pallas_call(attend_kernel, out_shape=jax.ShapeDtypeStruct((count, head...  7.99 us
  transfers between devices with their start and end apart: 1, of which 0 were waited for; matrix products, arithmetic and copies ran while one was open for 0% of the time, Pallas kernels for 5%

profile of v2, /device:TPU:1, one launch (start us, length us, event | category | flops | bytes accessed | tf_op | source)
XLA Modules:
  0.0 146.3 jit_solution(13232911401275374217)
XLA Ops:
  0.6 0.0 copy-start.2
  0.6 0.0 copy-start
  1.5 2.8 %prepare.1 = (bf16[64,2816]{1,0:T(8,128)(2,1)}, bf16[4,64,256]{2,1,0:T(8,128)(2,1)}, bf16[576,256]{1,0:T(8,128)(2,1)S(1)}) custom-call(s32[1]{0:T(128)} %bitcast.dev_ref, s32[128]{0:T(128)} %slot_ref.3, bf16[64,3584]{1,0:T(8,128)(2,1)} %x_ref.1, s32[8,64]{1,0:T(8,128)} %bitcast.37, f32[8,64]{1,0:T(8,128)} %bitcast.38, bf16[16,576,256]{2,1,0:T(8,128)(2,1)} %bitcast.27), custom_call_target="tpu_custom_call" | custom-call | tf_op jit(solution)/shard_map/prepare/pallas_call | solution.py:744
  4.3 0.0 copy-done.2
  4.3 0.0 copy-done
  4.3 10.2 %conditional.2 = (bf16[576,256]{1,0:T(8,128)(2,1)S(1)}, bf16[16,128,512]{2,1,0:T(8,128)(2,1)}) conditional(s32[]{:T(128)} %bitcast.9, (s32[1]{0:T(128)}, s32[2048]{0:T(1024)S(1)}, bf16[16,576,128]{2,1,0:T(8,128)(2,1)S(1)}, bf16[16,576,256]{2,1,0:T(8,128)(2,1)}, bf16[576,256]{1,0:T(8,128)(2,1)S(1)}) %tuple.99, ...), branch_computations={%region_0.0_spmd, %region_1.0_spmd, %region_2.0_spmd, %region_3.0_... | conditional | flops 2400000000 | bytes 21769528 | solution.py:709
  4.3 2.1 %collective-permute-start = (bf16[576,256]{1,0:T(8,128)(2,1)S(1)}, bf16[576,256]{1,0:T(8,128)(2,1)S(1)}, u32[]{:S(2)}, u32[]{:S(2)}) collective-permute-start(bf16[576,256]{1,0:T(8,128)(2,1)S(1)} %get-tuple-element.141), channel_id=1, source_target_pairs={{0,32},{4,36},{8,40},{12,44},{16,48},{20,52},{24,56},{28,60},{32,0... | collective-permute-start | bytes 884744 | tf_op jit(solution)/shard_map/cond/branch_1_fun/ppermute | solution.py:704
  6.4 8.0 %attend.5 = bf16[16,128,512]{2,1,0:T(8,128)(2,1)} custom-call(s32[1]{0:T(128)} %get-tuple-element.142.dev_ref, s32[2048]{0:T(1024)S(1)} %get-tuple-element.143.lens_ref, bf16[16,576,128]{2,1,0:T(8,128)(2,1)S(1)} %get-tuple-element.144.q_ref, bf16[16,576,256]{2,1,0:T(8,128)(2,1)} %get-tuple-element.145.page_ref), custom_call_target="tpu_custom_call" | custom-call | flops 2400000000 | bytes 20000000 | tf_op jit(solution)/shard_map/cond/branch_1_fun/attend/pallas_call | solution.py:655
  14.4 0.0 collective-permute-done
  14.4 49.9 %gather_rows.1 = (bf16[4,4,2,64,2816]{4,3,2,1,0:T(8,128)(2,1)}, bf16[4,4,4,2,64,256]{5,4,3,2,1,0:T(8,128)(2,1)}, bf16[3,256,1792]{2,1,0:T(8,128)(2,1)}) custom-call(bf16[64,2816]{1,0:T(8,128)(2,1)} %get-tuple-element.216.x_ref, bf16[4,64,256]{2,1,0:T(8,128)(2,1)} %get-tuple-element.217.xp_ref, bf16[3,256,3584]{2,1,0:T(8,128)(2,1)} %wd_hbm.1), custom_call_target="tpu_custom_call" | custom-call | tf_op jit(solution)/shard_map/gather_rows/pallas_call | solution.py:264
  64.4 17.5 %conditional.3 = (bf16[576,256]{1,0:T(8,128)(2,1)S(1)}, bf16[3,320,256]{2,1,0:T(8,128)(2,1)S(1)}) conditional(s32[]{:T(128)} %bitcast.2, (s32[1]{0:T(128)}, bf16[4,512,2816]{2,1,0:T(8,128)(2,1)}, bf16[4,4,512,256]{3,2,1,0:T(8,128)(2,1)}, bf16[3,3584,256]{2,1,0:T(8,128)(2,1)}, bf16[3,3584,256]{2,1,0:T(8,128)(2,1)}, ...), branch_computations={%region_4.0_spmd, %region_5.0_spmd, %region_6.0_spmd, %region_7.0_... | conditional | flops 7000000000 | bytes 31769528 | solution.py:709
  64.4 17.3 %experts_up.8 = bf16[3,320,256]{2,1,0:T(8,128)(2,1)S(1)} custom-call(s32[1]{0:T(128)} %get-tuple-element.157.base_ref, bf16[4,512,2816]{2,1,0:T(8,128)(2,1)} %get-tuple-element.158.x_ref, bf16[4,4,512,256]{3,2,1,0:T(8,128)(2,1)} %get-tuple-element.159.xp_ref, bf16[3,3584,256]{2,1,0:T(8,128)(2,1)} %get-tuple-element.160.wg_hbm, ...), custom_call_target="tpu_custom_call" | custom-call | flops 7000000000 | bytes 30000000 | tf_op jit(solution)/shard_map/cond/branch_0_fun/experts_up/pallas_call | solution.py:358
  81.9 61.8 %combine.1 = bf16[64,896]{1,0:T(8,128)(2,1)} custom-call(bf16[3,320,256]{2,1,0:T(8,128)(2,1)S(1)} %get-tuple-element.224.inner_ref, bf16[3,256,3584]{2,1,0:T(8,128)(2,1)} %wd_hbm.1, bf16[3,256,1792]{2,1,0:T(8,128)(2,1)} %get-tuple-element.225.wdp_hbm, bf16[4,512,2816]{2,1,0:T(8,128)(2,1)} %bitcast.18), custom_call_target="tpu_custom_call" | custom-call | tf_op jit(solution)/shard_map/combine/pallas_call | solution.py:598
  143.6 0.0 copy-start.1
  143.7 2.0 %attend_one.1 = bf16[16,128,512]{2,1,0:T(8,128)(2,1)} custom-call(s32[1]{0:T(128)} %bitcast.dev_ref, s32[128]{0:T(128)} %slot_ref.3, s32[1]{0:T(128)S(6)} %copy.40.mask_ref, s32[2048]{0:T(1024)S(1)} %copy-done.2, bf16[16,576,128]{2,1,0:T(8,128)(2,1)S(1)} %bitcast.36, ...), custom_call_target="tpu_custom_call", output_to_operand_aliasing={{}: (6, {})} | custom-call | tf_op jit(solution)/shard_map/attend_one/pallas_call | solution.py:680
  145.7 0.0 copy-done.1
  145.7 0.6 copy.41
  (1 shorter events, 0.0 us)
Async XLA Ops:
  0.6 3.6 %copy-start.2 = (s32[2048]{0:T(1024)S(1)}, s32[2048]{0:T(1024)}, u32[]{:S(2)}) copy-start(s32[2048]{0:T(1024)} %lens_ref.1) | copy-start | bytes 24580
  0.6 3.6 %copy-start = (bf16[16,128,576]{1,2,0:T(8,128)(2,1)S(1)}, bf16[16,128,576]{1,2,0:T(8,128)(2,1)}, u32[]{:S(2)}) copy-start(bf16[16,128,576]{1,2,0:T(8,128)(2,1)} %param.24) | copy-start | bytes 7077892
  4.3 10.1 %collective-permute-start = (bf16[576,256]{1,0:T(8,128)(2,1)S(1)}, bf16[576,256]{1,0:T(8,128)(2,1)S(1)}, u32[]{:S(2)}, u32[]{:S(2)}) collective-permute-start(bf16[576,256]{1,0:T(8,128)(2,1)S(1)} %get-tuple-element.141), channel_id=1, source_target_pairs={{0,32},{4,36},{8,40},{12,44},{16,48},{20,52},{24,56},{28,60},{32,0... | collective-permute-start | bytes 884744 | tf_op jit(solution)/shard_map/cond/branch_1_fun/ppermute | solution.py:704
  143.6 2.0 %copy-start.1 = (bf16[64,896]{1,0:T(8,128)(2,1)S(1)}, bf16[64,896]{1,0:T(8,128)(2,1)}, u32[]{:S(2)}) copy-start(bf16[64,896]{1,0:T(8,128)(2,1)} %combine.1) | copy-start | bytes 344068

commit v3 on v2

--- a/solution.py
+++ b/solution.py
@@ -16,8 +16,11 @@
 CAP = 10
 EXL = 3
 META = 256
-GROUP = 512
-GSLOT = 80
+GROUP = 256
+GROUPS = 8
+GSLOT = 40
+PAIR = 2 * GROUP
+PSLOT = 2 * GSLOT
 HALF = D // 2
 BLK = D // 4
 FFL = 256
@@ -199,10 +202,10 @@
         + [other, above, below]
     )
     open1(0)
-    open1(1)
     far = pl.ds(pl.multiple_of((1 - c) * HALF, HALF), HALF)
     push(wd_ref.at[:, :, far], wdp_ref, other, wsem.at[0], wsem.at[1])
     relay1(0)
+    open1(1)
     locals_[0].wait()
     for col in (0, 1):
         last1(0, col)
@@ -254,7 +257,8 @@
     for d in range(4):
         expect(part_of(wrap(y + d), 0, 4, 1 - c), ydrecv.at[d])
     expect(wdp_ref, wsem.at[1])
-    locals_[1].wait()
+    for copy in locals_[1:]:
+        copy.wait()
     for copy in started:
         copy.wait_send()
 
@@ -266,10 +270,11 @@
         out_shape=(
             jax.ShapeDtypeStruct((4, 4, 2, ROWS, WHOLE), BF),
             jax.ShapeDtypeStruct((4, 4, 4, 2, ROWS, QUARTER), BF),
-            jax.ShapeDtypeStruct((EXL, FFL, HALF), BF),
+            pltpu.HBM((EXL, FFL, HALF), BF),
         ),
-        in_specs=[pl.BlockSpec(memory_space=pltpu.VMEM)] * 2 + [pl.BlockSpec(memory_space=pl.ANY)],
-        out_specs=(pl.BlockSpec(memory_space=pl.ANY),) * 3,
+        in_specs=[pl.BlockSpec(memory_space=pltpu.VMEM)] * 2 + [pl.BlockSpec(memory_space=pltpu.HBM)],
+        out_specs=(pl.BlockSpec(memory_space=pltpu.VMEM),) * 2
+        + (pl.BlockSpec(memory_space=pltpu.HBM),),
         scratch_shapes=[
             dma((2, 2, 20)),
             dma((2, 2, 4)),
@@ -284,108 +289,96 @@
             dma((2,)),
         ],
         compiler_params=pltpu.CompilerParams(
-            collective_id=0, has_side_effects=True, vmem_limit_bytes=VMEM_MAX
+            collective_id=0, has_side_effects=True, vmem_limit_bytes=18 * 1024 * 1024
         ),
         name="gather_rows",
     )(xmain, xparts, w_down)
 
 
-def slot_numbers(shape, axis):
+def slot_numbers(shape, axis, gslot):
     s = lax.broadcasted_iota(jnp.int32, shape, axis)
     g = lax.broadcasted_iota(jnp.int32, shape, 1 - axis)
     expert = jnp.zeros(shape, jnp.int32)
-    for k in range(1, shape[axis] // GSLOT):
-        expert = expert + (s >= k * GSLOT).astype(jnp.int32)
-    u = s - expert * GSLOT
+    for k in range(1, shape[axis] // gslot):
+        expert = expert + (s >= k * gslot).astype(jnp.int32)
+    u = s - expert * gslot
     rank = (u * 205) >> 11
     want = jnp.where((g >> 6) == rank, u - rank * CAP + 1, -1)
     return want.astype(F32)
 
 
-def expert_lanes(shape, axis, base):
+def expert_lanes(shape, axis, base, gslot):
     s = lax.broadcasted_iota(jnp.int32, shape, axis)
     e = lax.broadcasted_iota(jnp.int32, shape, 1 - axis)
     expert = jnp.zeros(shape, jnp.int32)
-    for k in range(1, shape[axis] // GSLOT):
-        expert = expert + (s >= k * GSLOT).astype(jnp.int32)
+    for k in range(1, shape[axis] // gslot):
+        expert = expert + (s >= k * gslot).astype(jnp.int32)
     return jnp.where(expert + base == e, 1.0, 0.0).astype(BF)
 
 
-def up_kernel(base_ref, x_ref, xp_ref, wg_hbm, wu_hbm, out_ref, xc, want, lanes, wg, wu, sem):
-    q = pl.program_id(0)
-    gate_copy = pltpu.make_async_copy(wg_hbm, wg, sem.at[0])
-    up_copy = pltpu.make_async_copy(wu_hbm, wu, sem.at[1])
-
-    @pl.when(q == 0)
-    def _():
-        gate_copy.start()
-        up_copy.start()
-        want[...] = slot_numbers((EXL * GSLOT, GROUP), 0)
-        lanes[...] = expert_lanes((EXL * GSLOT, 128), 0, base_ref[0])
-
-    table = x_ref[0, :, MAIN : MAIN + 128]
-    named = lax.dot_general(lanes[...], table, (((1,), (1,)), ((), ())), preferred_element_type=F32)
-    pick = jnp.where(named == want[...], 1.0, 0.0).astype(BF)
-    start = pl.multiple_of(q * GSLOT, 16)
-
-    def keep(rows, cols):
-        for e in range(EXL):
-            xc[e, pl.ds(start, GSLOT), cols] = rows[e * GSLOT : (e + 1) * GSLOT].astype(BF)
-
-    @pl.loop(0, MAIN // 512)
-    def _(n):
-        cols = pl.ds(pl.multiple_of(n * 512, 512), 512)
-        keep(jnp.dot(pick, x_ref[0, :, cols], preferred_element_type=F32), cols)
-
-    @pl.loop(0, 4)
-    def _(n):
-        cols = pl.ds(pl.multiple_of(MAIN + n * QUARTER, 128), QUARTER)
-        keep(jnp.dot(pick, xp_ref[n, 0], preferred_element_type=F32), cols)
-
-    @pl.when(q == 3)
-    def _():
-        gate_copy.wait()
-        up_copy.wait()
-
-        @pl.loop(0, EXL)
-        def _(e):
-            gate = jnp.dot(xc[e], wg[e], preferred_element_type=F32)
-            up = jnp.dot(xc[e], wu[e], preferred_element_type=F32)
-            out_ref[e] = (gate / (1.0 + jnp.exp(-gate)) * up).astype(BF)
+def up_kernel(base_ref, x_ref, xp_ref, wg_ref, wu_hbm, out_ref, tab_ref, xc, wu_ref, sem):
+    load = pltpu.make_async_copy(wu_hbm, wu_ref, sem)
+    load.start()
+    tab_ref[...] = x_ref[:, :, MAIN:WHOLE]
+    want = slot_numbers((EXL * PSLOT, PAIR), 0, PSLOT)
+    lanes = expert_lanes((EXL * PSLOT, 128), 0, base_ref[0], PSLOT)
+
+    @pl.loop(0, GROUPS // 2)
+    def _(q):
+        table = x_ref[q, :, MAIN : MAIN + 128]
+        named = lax.dot_general(lanes, table, (((1,), (1,)), ((), ())), preferred_element_type=F32)
+        pick = jnp.where(named == want, 1.0, 0.0).astype(BF)
+        start = pl.multiple_of(q * PSLOT, 16)
+
+        def keep(rows, cols):
+            for e in range(EXL):
+                xc[e, pl.ds(start, PSLOT), cols] = rows[e * PSLOT : (e + 1) * PSLOT].astype(BF)
+
+        @pl.loop(0, MAIN // 512)
+        def _(n):
+            cols = pl.ds(pl.multiple_of(n * 512, 512), 512)
+            keep(jnp.dot(pick, x_ref[q, :, cols], preferred_element_type=F32), cols)
+
+        @pl.loop(0, 4)
+        def _(n):
+            cols = pl.ds(pl.multiple_of(MAIN + n * QUARTER, 128), QUARTER)
+            keep(jnp.dot(pick, xp_ref[n, q], preferred_element_type=F32), cols)
+
+    load.wait()
+
+    @pl.loop(0, EXL)
+    def _(e):
+        rows = xc[e]
+        gate = jnp.dot(rows, wg_ref[e], preferred_element_type=F32)
+        up = jnp.dot(rows, wu_ref[e], preferred_element_type=F32)
+        out_ref[e] = (gate / (1.0 + jnp.exp(-gate)) * up).astype(BF)
 
 
 def experts_up(base, xg, xq, w_gate, w_up):
     return pl.pallas_call(
         up_kernel,
-        out_shape=jax.ShapeDtypeStruct((EXL, 4 * GSLOT, FFL), BF),
-        grid_spec=pltpu.PrefetchScalarGridSpec(
-            num_scalar_prefetch=1,
-            grid=(4,),
-            in_specs=[
-                pl.BlockSpec((1, GROUP, WHOLE), lambda q, b: (q, 0, 0)),
-                pl.BlockSpec((4, 1, GROUP, QUARTER), lambda q, b: (0, q, 0, 0)),
-                pl.BlockSpec(memory_space=pl.ANY),
-                pl.BlockSpec(memory_space=pl.ANY),
-            ],
-            out_specs=pl.BlockSpec((EXL, 4 * GSLOT, FFL), lambda q, b: (0, 0, 0)),
-            scratch_shapes=[
-                pltpu.VMEM((EXL, 4 * GSLOT, D), BF),
-                pltpu.VMEM((EXL * GSLOT, GROUP), F32),
-                pltpu.VMEM((EXL * GSLOT, 128), BF),
-                pltpu.VMEM((EXL, D, FFL), BF),
-                pltpu.VMEM((EXL, D, FFL), BF),
-                pltpu.SemaphoreType.DMA((2,)),
-            ],
+        out_shape=(
+            jax.ShapeDtypeStruct((EXL, GROUPS * GSLOT, FFL), BF),
+            jax.ShapeDtypeStruct((GROUPS // 2, PAIR, META), BF),
         ),
+        in_specs=[pl.BlockSpec(memory_space=pltpu.SMEM)]
+        + [pl.BlockSpec(memory_space=pltpu.VMEM)] * 3
+        + [pl.BlockSpec(memory_space=pltpu.HBM)],
+        out_specs=(pl.BlockSpec(memory_space=pltpu.VMEM),) * 2,
+        scratch_shapes=[
+            pltpu.VMEM((EXL, GROUPS * GSLOT, D), BF),
+            pltpu.VMEM((EXL, D, FFL), BF),
+            pltpu.SemaphoreType.DMA,
+        ],
         cost_estimate=pl.CostEstimate(flops=7_000_000_000, bytes_accessed=30_000_000, transcendentals=0),
-        compiler_params=pltpu.CompilerParams(vmem_limit_bytes=VMEM_MAX),
+        compiler_params=pltpu.CompilerParams(vmem_limit_bytes=20 * 1024 * 1024),
         name="experts_up",
     )(base, xg, xq, w_gate, w_up)
 
 
 def combine_kernel(
-    inner_ref, wd_hbm, wdp_hbm, xg_hbm, out_ref,
-    inner2, wdh, meta, outc, want, yp, st1, fin1, st2, fin2, fin3,
+    inner_ref, meta, wd_hbm, wdp_hbm, out_ref,
+    inner2, wdh, outc, want, yp, st1, fin1, st2, fin2, fin3,
     lsem, isem, s1, r1, s2, r2, s3, r3,
 ):
     x, z, c, y = coords()
@@ -411,12 +404,11 @@
     loads = [
         pltpu.make_async_copy(wd_hbm.at[:, :, near], wdh.at[c], lsem.at[0]),
         pltpu.make_async_copy(wdp_hbm, wdh.at[1 - c], lsem.at[1]),
-        pltpu.make_async_copy(xg_hbm.at[:, :, pl.ds(MAIN, META)], meta, lsem.at[2]),
     ]
     for load in loads:
         load.start()
-    want[...] = slot_numbers((GROUP, 2 * EXL * GSLOT), 1)
-    lanes = expert_lanes((128, 2 * EXL * GSLOT), 1, (x * 4 + z) * 2 * EXL)
+    want[...] = slot_numbers((GROUP, 2 * EXL * GSLOT), 1, GSLOT)
+    lanes = expert_lanes((128, 2 * EXL * GSLOT), 1, (x * 4 + z) * 2 * EXL, GSLOT)
     greet(
         [dev(wrap(x + 1), z, c, y), dev(wrap(x - 1), z, c, y), dev(x, wrap(z + 1), c, y), dev(x, wrap(z - 1), c, y)]
         + [other]
@@ -427,11 +419,11 @@
     def down(core, source):
         @pl.loop(0, EXL)
         def _(e):
-            row = pl.multiple_of((core * EXL + e) * GSLOT, 16)
+            row = pl.multiple_of((core * EXL + e) * GSLOT, 8)
             for n in range(2):
                 cols = slice(n * BLK, (n + 1) * BLK)
-                part = jnp.dot(source[e], wdh[core, e, :, cols], preferred_element_type=F32).astype(BF)
-                for q in range(4):
+                part = jnp.dot(source[e], wdh[core, e, :, cols], preferred_element_type=F32)
+                for q in range(GROUPS):
                     outc[n, q, pl.ds(row, GSLOT), :] = part[q * GSLOT : (q + 1) * GSLOT]
 
     loads[0].wait()
@@ -439,21 +431,23 @@
     loads[1].wait()
     swap.wait_recv()
     down(1 - c, inner2)
-    loads[2].wait()
-
-    def scatter(col):
-        @pl.loop(0, 4)
-        def _(q):
+
+    def scatter(col, start, count):
+        @pl.loop(0, 2 * count)
+        def _(i):
+            q = wrap(x + start + i // 2) * 2 + lax.rem(i, 2)
             named = jnp.dot(meta[q, :, 0:128], lanes, preferred_element_type=F32)
             gate = jnp.dot(meta[q, :, 128:256], lanes, preferred_element_type=F32)
             mix = jnp.where(named == want[...], gate, 0.0).astype(BF)
-            part = jnp.dot(mix, outc[col, q], preferred_element_type=F32).astype(BF)
-            for k in range(4):
+            part = jnp.dot(mix, outc[col, q].astype(BF), preferred_element_type=F32).astype(BF)
+            xx = q // 2
+            for k in range(2):
                 piece = part[k * 128 : (k + 1) * 128]
+                zz = lax.rem(q, 2) * 2 + k
                 if col == 0:
-                    yp[0, q, k] = piece
+                    yp[0, xx, zz] = piece
                 else:
-                    yp[1, k, q] = piece
+                    yp[1, zz, xx] = piece
 
     first, second = (x, z), (z, x)
 
@@ -463,11 +457,15 @@
     def sdev(col, s):
         return dev(x, s, c, y) if col == 0 else dev(s, z, c, y)
 
-    def open1(col):
+    def open0(col):
         p = first[col]
         up, dn = fdev(col, wrap(p + 1)), fdev(col, wrap(p - 1))
         ship(yp.at[col, wrap(p + 2), pl.ds(0, 2)], st1.at[col, 0], up, s1.at[col, 0], r1.at[col, 0])
         ship(yp.at[col, wrap(p + 2), pl.ds(2, 2)], st1.at[col, 1], dn, s1.at[col, 1], r1.at[col, 1])
+
+    def open1(col):
+        p = first[col]
+        up, dn = fdev(col, wrap(p + 1)), fdev(col, wrap(p - 1))
         ship(yp.at[col, wrap(p + 1), pl.ds(2, 2)], fin1.at[col, 0, pl.ds(2, 2)], up, s1.at[col, 2], r1.at[col, 2])
         ship(yp.at[col, wrap(p - 1), pl.ds(0, 2)], fin1.at[col, 1, pl.ds(0, 2)], dn, s1.at[col, 3], r1.at[col, 3])
 
@@ -570,12 +568,15 @@
                 acc = acc + fin3[k].astype(F32)
             out_ref[...] = acc.astype(BF)
 
-    scatter(0)
+    scatter(1, 0, 4)
+    open0(1)
+    open1(1)
+    scatter(0, 2, 1)
+    open0(0)
+    scatter(0, 3, 3)
     open1(0)
-    scatter(1)
-    open1(1)
     for step in (mid1, end1, mid2, end2):
-        for col in (0, 1):
+        for col in (1, 0):
             step(col)
     for k in (1, 2, 3):
         expect(fin3.at[k], r3.at[k])
@@ -594,17 +595,16 @@
         copy.wait_send()
 
 
-def combine(inner, w_down, wd_far, xg):
+def combine(inner, tables, w_down, wd_far):
     return pl.pallas_call(
         combine_kernel,
         out_shape=jax.ShapeDtypeStruct((ROWS, BLK), BF),
-        in_specs=[pl.BlockSpec(memory_space=pltpu.VMEM)] + [pl.BlockSpec(memory_space=pl.ANY)] * 3,
+        in_specs=[pl.BlockSpec(memory_space=pltpu.VMEM)] * 2 + [pl.BlockSpec(memory_space=pltpu.HBM)] * 2,
         out_specs=pl.BlockSpec(memory_space=pltpu.VMEM),
         scratch_shapes=[
-            pltpu.VMEM((EXL, 4 * GSLOT, FFL), BF),
+            pltpu.VMEM((EXL, GROUPS * GSLOT, FFL), BF),
             pltpu.VMEM((2, EXL, FFL, HALF), BF),
-            pltpu.VMEM((4, GROUP, META), BF),
-            pltpu.VMEM((2, 4, 2 * EXL * GSLOT, BLK), BF),
+            pltpu.VMEM((2, GROUPS, 2 * EXL * GSLOT, BLK), F32),
             pltpu.VMEM((GROUP, 2 * EXL * GSLOT), F32),
             pltpu.VMEM((2, 4, 4, 128, BLK), BF),
             pltpu.VMEM((2, 2, 2, 128, BLK), BF),
@@ -612,7 +612,7 @@
             pltpu.VMEM((2, 2, 64, BLK), BF),
             pltpu.VMEM((2, 2, 128, BLK), BF),
             pltpu.VMEM((4, 64, BLK), BF),
-            pltpu.SemaphoreType.DMA((3,)),
+            pltpu.SemaphoreType.DMA((2,)),
             pltpu.SemaphoreType.DMA((2,)),
             pltpu.SemaphoreType.DMA((2, 6)),
             pltpu.SemaphoreType.DMA((2, 6)),
@@ -622,10 +622,10 @@
             pltpu.SemaphoreType.DMA((4,)),
         ],
         compiler_params=pltpu.CompilerParams(
-            collective_id=1, has_side_effects=True, vmem_limit_bytes=VMEM_MAX
+            collective_id=1, has_side_effects=True, vmem_limit_bytes=38 * 1024 * 1024
         ),
         name="combine",
-    )(inner, w_down, wd_far, xg)
+    )(inner, tables, w_down, wd_far)
 
 
 def attend_page(query, page, length):
@@ -633,12 +633,12 @@
     scores = scores * SCORE_SCALE
     live = lax.broadcasted_iota(jnp.int32, scores.shape, 1) < length
     scores = jnp.where(live, scores, MASK_FLOOR)
-    weight = jnp.where(live, jnp.exp(scores - jnp.max(scores, axis=1, keepdims=True)), 0.0)
+    weight = jnp.exp(scores - jnp.max(scores, axis=1, keepdims=True))
     total = jnp.sum(weight, axis=1, keepdims=True)
     blended = lax.dot_general(
         weight.astype(BF), page[:LAT], (((1,), (1,)), ((), ())), preferred_element_type=F32
     )
-    return (blended / total).astype(BF)
+    return (blended * (1.0 / total)).astype(BF)
 
 
 def attend_kernel(dev_ref, lens_ref, q_ref, page_ref, out_ref):
@@ -788,18 +788,19 @@
     dev = device.reshape(1)
     pages = jnp.swapaxes(cache_pages, 1, 2)
     asked = jnp.swapaxes(queries, 1, 2)
+    w_down = pltpu.with_memory_space_constraint(w_down, pltpu.HBM)
     xmain, xparts, own_page = prepare(dev, swap_slot, hidden, expert_ids.T, gate_weights.T, pages)
     page, attended = trade(
         own_page, jnp.right_shift(mask, 3), 3, 4, lambda: attend(dev, lengths, asked, pages)
     )
     xg, xq, wd_far = gather_rows(xmain, xparts, w_down)
-    xg = xg.reshape(4, GROUP, WHOLE)
-    xq = xq.reshape(4, 4, GROUP, QUARTER)
+    xg = xg.reshape(GROUPS // 2, PAIR, WHOLE)
+    xq = xq.reshape(4, GROUPS // 2, PAIR, QUARTER)
     base = (ep_rank * EXL).reshape(1)
-    page, inner = trade(
+    page, (inner, tables) = trade(
         page, jnp.bitwise_and(mask, 7), 0, 8, lambda: experts_up(base, xg, xq, w_gate, w_up)
     )
-    moe_rows = combine(inner, w_down, wd_far, xg)
+    moe_rows = combine(inner, tables.reshape(GROUPS, GROUP, META), w_down, wd_far)
     attended = attend_one(dev, swap_slot, swap_mask, lengths, asked, page, attended)
     return attended, moe_rows
 

time: 147 us -> 142 us (0.966)
  Pallas kernels: 142 us -> 136 us
    pallas_call x1, Pallas kernels: 17.3 us -> 14.9 us  [experts_up(): pl.pallas_call(up_kernel, out_shape=(jax.ShapeDtypeStruct((EXL, GROUPS *...]
    pallas_call x1, Pallas kernels: 49.9 us -> 47.8 us  [gather_rows(): pl.pallas_call(gather_kernel, out_shape=(jax.ShapeDtypeStruct((4, 4, 2, R...]
    pallas_call x1, Pallas kernels: 61.8 us -> 60.1 us  [combine(): pl.pallas_call(combine_kernel, out_shape=jax.ShapeDtypeStruct((ROWS, BLK)...]
  transfers between devices with their start and end apart: 1 -> 1, of which waited for: 0 -> 0; matrix products, arithmetic and copies ran while one was open for 0% -> 0% of each run, Pallas kernels for 5% -> 6%
where the time goes in v3:
time: 142 us
  Pallas kernels  136 us (96%)
  starting transfers between devices  2.11 us (1%)
  between operations  1.53 us (1%)
    pallas_call x1, Pallas kernels, combine(): pl.pallas_call(combine_kernel, out_shape=jax.ShapeDtypeStruct((ROWS, BLK)...  60.1 us
    pallas_call x1, Pallas kernels, gather_rows(): pl.pallas_call(gather_kernel, out_shape=(jax.ShapeDtypeStruct((4, 4, 2, R...  47.8 us
    pallas_call x1, Pallas kernels, experts_up(): pl.pallas_call(up_kernel, out_shape=(jax.ShapeDtypeStruct((EXL, GROUPS *...  14.9 us
    pallas_call x1, Pallas kernels, attend(): pl.pallas_call(attend_kernel, out_shape=jax.ShapeDtypeStruct((count, head...  8 us
    pallas_call x1, Pallas kernels, attend_one(): pl.pallas_call(attend_one_kernel, out_shape=jax.ShapeDtypeStruct(attended...  2.88 us
  transfers between devices with their start and end apart: 1, of which 0 were waited for; matrix products, arithmetic and copies ran while one was open for 0% of the time, Pallas kernels for 6%

profile of v3, /device:TPU:1, one launch (start us, length us, event | category | flops | bytes accessed | tf_op | source)
XLA Modules:
  0.0 141.7 jit_solution(565484211361222140)
XLA Ops:
  0.6 0.0 copy-start.5
  0.6 0.0 copy-start.4
  1.5 2.8 %prepare.1 = (bf16[64,2816]{1,0:T(8,128)(2,1)}, bf16[4,64,256]{2,1,0:T(8,128)(2,1)}, bf16[576,256]{1,0:T(8,128)(2,1)}) custom-call(s32[1]{0:T(128)} %bitcast.dev_ref, s32[128]{0:T(128)} %slot_ref.3, bf16[64,3584]{1,0:T(8,128)(2,1)} %x_ref.1, s32[8,64]{1,0:T(8,128)} %bitcast.38, f32[8,64]{1,0:T(8,128)} %bitcast.39, bf16[16,576,256]{2,1,0:T(8,128)(2,1)} %bitcast.27), custom_call_target="tpu_custom_call" | custom-call | tf_op jit(solution)/shard_map/prepare/pallas_call | solution.py:744
  4.3 0.0 copy-done.5
  4.3 0.0 copy-done.4
  4.3 0.0 copy-start.1
  4.3 0.0 copy-start.2
  4.3 10.8 %conditional.2 = (bf16[576,256]{1,0:T(8,128)(2,1)}, bf16[16,128,512]{2,1,0:T(8,128)(2,1)}) conditional(s32[]{:T(128)} %bitcast.9, (s32[1]{0:T(128)}, s32[2048]{0:T(1024)S(1)}, bf16[16,576,128]{2,1,0:T(8,128)(2,1)S(1)}, bf16[16,576,256]{2,1,0:T(8,128)(2,1)}, bf16[576,256]{1,0:T(8,128)(2,1)}) %tuple.107, ...), branch_computations={%region_0.0_spmd, %region_1.0_spmd, %region_2.0_spmd, %region_3.0_... | conditional | flops 2400000000 | bytes 21769528 | solution.py:709
  4.3 2.1 %collective-permute-start = (bf16[576,256]{1,0:T(8,128)(2,1)}, bf16[576,256]{1,0:T(8,128)(2,1)S(1)}, u32[]{:S(2)}, u32[]{:S(2)}) collective-permute-start(bf16[576,256]{1,0:T(8,128)(2,1)} %get-tuple-element.141), channel_id=1, source_target_pairs={{0,32},{4,36},{8,40},{12,44},{16,48},{20,52},{24,56},{28,60},{32,0... | collective-permute-start | bytes 884744 | tf_op jit(solution)/shard_map/cond/branch_1_fun/ppermute | solution.py:704
  6.4 8.0 %attend.5 = bf16[16,128,512]{2,1,0:T(8,128)(2,1)} custom-call(s32[1]{0:T(128)} %get-tuple-element.142.dev_ref, s32[2048]{0:T(1024)S(1)} %get-tuple-element.143.lens_ref, bf16[16,576,128]{2,1,0:T(8,128)(2,1)S(1)} %get-tuple-element.144.q_ref, bf16[16,576,256]{2,1,0:T(8,128)(2,1)} %get-tuple-element.145.page_ref), custom_call_target="tpu_custom_call" | custom-call | flops 2400000000 | bytes 20000000 | tf_op jit(solution)/shard_map/cond/branch_1_fun/attend/pallas_call | solution.py:655
  14.4 0.0 collective-permute-done
  14.4 0.7 copy.16
  15.1 0.0 copy-done.1
  15.1 0.0 copy-done.2
  15.1 0.0 copy-start.3
  15.1 47.8 %gather_rows.1 = (bf16[4,4,2,64,2816]{4,3,2,1,0:T(8,128)(2,1)S(1)}, bf16[4,4,4,2,64,256]{5,4,3,2,1,0:T(8,128)(2,1)S(1)}, bf16[3,256,1792]{2,1,0:T(8,128)(2,1)}) custom-call(bf16[64,2816]{1,0:T(8,128)(2,1)S(1)} %copy-done.1, bf16[4,64,256]{2,1,0:T(8,128)(2,1)S(1)} %copy-done.2, bf16[3,256,3584]{2,1,0:T(8,128)(2,1)} %wd_hbm.1), custom_call_target="tpu_custom_call" | custom-call | tf_op jit(solution)/shard_map/gather_rows/pallas_call | solution.py:268
  62.9 0.0 copy-done.3
  62.9 0.0 copy-start
  62.9 15.1 %conditional.3 = (bf16[576,256]{1,0:T(8,128)(2,1)}, bf16[3,320,256]{2,1,0:T(8,128)(2,1)S(1)}, bf16[4,512,256]{2,1,0:T(8,128)(2,1)S(1)}) conditional(s32[]{:T(128)} %bitcast.2, (s32[1]{0:T(128)}, bf16[4,512,2816]{2,1,0:T(8,128)(2,1)S(1)}, bf16[4,4,512,256]{3,2,1,0:T(8,128)(2,1)S(1)}, ...), branch_computations={%region_4.0_spmd, %region_5.0_spmd, %region_6.0_spmd, %region_7.0_... | conditional | flops 7000000000 | bytes 31769536 | solution.py:709
  63.0 14.9 %experts_up.8 = (bf16[3,320,256]{2,1,0:T(8,128)(2,1)S(1)}, bf16[4,512,256]{2,1,0:T(8,128)(2,1)S(1)}) custom-call(s32[1]{0:T(128)} %get-tuple-element.157.base_ref, bf16[4,512,2816]{2,1,0:T(8,128)(2,1)S(1)} %get-tuple-element.158.x_ref, bf16[4,4,512,256]{3,2,1,0:T(8,128)(2,1)S(1)} %get-tuple-element.159.xp_ref, ...), custom_call_target="tpu_custom_call" | custom-call | flops 7000000000 | bytes 30000000 | tf_op jit(solution)/shard_map/cond/branch_0_fun/experts_up/pallas_call | solution.py:358
  78.1 0.0 copy-done
  78.1 60.1 %combine.1 = bf16[64,896]{1,0:T(8,128)(2,1)S(1)} custom-call(bf16[3,320,256]{2,1,0:T(8,128)(2,1)S(1)} %get-tuple-element.241.inner_ref, bf16[8,256,256]{2,1,0:T(8,128)(2,1)S(1)} %bitcast.37, bf16[3,256,3584]{2,1,0:T(8,128)(2,1)} %wd_hbm.1, bf16[3,256,1792]{2,1,0:T(8,128)(2,1)S(1)} %copy-done), custom_call_target="tpu_custom_call" | custom-call | tf_op jit(solution)/shard_map/combine/pallas_call | solution.py:599
  138.2 2.9 %attend_one.1 = bf16[16,128,512]{2,1,0:T(8,128)(2,1)} custom-call(s32[1]{0:T(128)} %bitcast.dev_ref, s32[128]{0:T(128)} %slot_ref.3, s32[1]{0:T(128)S(6)} %copy.48.mask_ref, s32[2048]{0:T(1024)S(1)} %copy-done.5, bf16[16,576,128]{2,1,0:T(8,128)(2,1)} %bitcast.32, bf16[576,256]{1,0:T(8,128)(2,1)} %get-tuple-element.239.page_ref, ...), custom_call_target="tpu_custom_call", output_to_operand_aliasing={{}: (6, {})} | custom-call | tf_op jit(solution)/shard_map/attend_one/pallas_call | solution.py:680
  141.1 0.6 copy.49
Async XLA Ops:
  0.6 3.6 %copy-start.5 = (s32[2048]{0:T(1024)S(1)}, s32[2048]{0:T(1024)}, u32[]{:S(2)}) copy-start(s32[2048]{0:T(1024)} %lens_ref.1) | copy-start | bytes 24580
  0.6 3.6 %copy-start.4 = (bf16[16,128,576]{1,2,0:T(8,128)(2,1)S(1)}, bf16[16,128,576]{1,2,0:T(8,128)(2,1)}, u32[]{:S(2)}) copy-start(bf16[16,128,576]{1,2,0:T(8,128)(2,1)} %param.24) | copy-start | bytes 7077892
  4.3 10.9 %copy-start.1 = (bf16[64,2816]{1,0:T(8,128)(2,1)S(1)}, bf16[64,2816]{1,0:T(8,128)(2,1)}, u32[]{:S(2)}) copy-start(bf16[64,2816]{1,0:T(8,128)(2,1)} %get-tuple-element.233.x_ref) | copy-start | bytes 1081348
  4.3 10.9 %copy-start.2 = (bf16[4,64,256]{2,1,0:T(8,128)(2,1)S(1)}, bf16[4,64,256]{2,1,0:T(8,128)(2,1)}, u32[]{:S(2)}) copy-start(bf16[4,64,256]{2,1,0:T(8,128)(2,1)} %get-tuple-element.234.xp_ref) | copy-start | bytes 393220
  4.3 10.1 %collective-permute-start = (bf16[576,256]{1,0:T(8,128)(2,1)}, bf16[576,256]{1,0:T(8,128)(2,1)S(1)}, u32[]{:S(2)}, u32[]{:S(2)}) collective-permute-start(bf16[576,256]{1,0:T(8,128)(2,1)} %get-tuple-element.141), channel_id=1, source_target_pairs={{0,32},{4,36},{8,40},{12,44},{16,48},{20,52},{24,56},{28,60},{32,0... | collective-permute-start | bytes 884744 | tf_op jit(solution)/shard_map/cond/branch_1_fun/ppermute | solution.py:704
  15.1 47.8 %copy-start.3 = (bf16[3,3584,256]{2,1,0:T(8,128)(2,1)S(1)}, bf16[3,3584,256]{2,1,0:T(8,128)(2,1)}, u32[]{:S(2)}) copy-start(bf16[3,3584,256]{2,1,0:T(8,128)(2,1)} %param.31) | copy-start | bytes 16515076
  62.9 15.2 %copy-start = (bf16[3,256,1792]{2,1,0:T(8,128)(2,1)S(1)}, bf16[3,256,1792]{2,1,0:T(8,128)(2,1)}, u32[]{:S(2)}) copy-start(bf16[3,256,1792]{2,1,0:T(8,128)(2,1)} %get-tuple-element.243.wdp_hbm) | copy-start | bytes 8257540

commit v4 on v3

--- a/solution.py
+++ b/solution.py
@@ -334,14 +334,11 @@
             for e in range(EXL):
                 xc[e, pl.ds(start, PSLOT), cols] = rows[e * PSLOT : (e + 1) * PSLOT].astype(BF)
 
-        @pl.loop(0, MAIN // 512)
-        def _(n):
-            cols = pl.ds(pl.multiple_of(n * 512, 512), 512)
+        for n in range(MAIN // 512):
+            cols = slice(n * 512, (n + 1) * 512)
             keep(jnp.dot(pick, x_ref[q, :, cols], preferred_element_type=F32), cols)
-
-        @pl.loop(0, 4)
-        def _(n):
-            cols = pl.ds(pl.multiple_of(MAIN + n * QUARTER, 128), QUARTER)
+        for n in range(4):
+            cols = slice(MAIN + n * QUARTER, MAIN + (n + 1) * QUARTER)
             keep(jnp.dot(pick, xp_ref[n, q], preferred_element_type=F32), cols)
 
     load.wait()
@@ -433,7 +430,7 @@
     down(1 - c, inner2)
 
     def scatter(col, start, count):
-        @pl.loop(0, 2 * count)
+        @pl.loop(0, 2 * count, unroll=2)
         def _(i):
             q = wrap(x + start + i // 2) * 2 + lax.rem(i, 2)
             named = jnp.dot(meta[q, :, 0:128], lanes, preferred_element_type=F32)

time: 142 us -> 136 us (0.958)
  Pallas kernels: 136 us -> 130 us
    pallas_call x1, Pallas kernels: 14.9 us -> 9.02 us  [experts_up(): pl.pallas_call(up_kernel, out_shape=(jax.ShapeDtypeStruct((EXL, GROUPS *...]
where the time goes in v4:
time: 136 us; the launch traced here: 135 us
  Pallas kernels  130 us (96%)
  starting transfers between devices  2.11 us (2%)
  between operations  1.53 us (1%)
  local copies, waits for them, and re-layouts  1.38 us (1%)
    pallas_call x1, Pallas kernels, combine(): pl.pallas_call(combine_kernel, out_shape=jax.ShapeDtypeStruct((ROWS, BLK)...  59.4 us
    pallas_call x1, Pallas kernels, gather_rows(): pl.pallas_call(gather_kernel, out_shape=(jax.ShapeDtypeStruct((4, 4, 2, R...  47.8 us
    pallas_call x1, Pallas kernels, experts_up(): pl.pallas_call(up_kernel, out_shape=(jax.ShapeDtypeStruct((EXL, GROUPS *...  9.02 us
    pallas_call x1, Pallas kernels, attend(): pl.pallas_call(attend_kernel, out_shape=jax.ShapeDtypeStruct((count, head...  8 us
    pallas_call x1, Pallas kernels, attend_one(): pl.pallas_call(attend_one_kernel, out_shape=jax.ShapeDtypeStruct(attended...  2.88 us
    pallas_call x1, Pallas kernels, prepare(): pl.pallas_call(prepare_kernel, out_shape=(jax.ShapeDtypeStruct((ROWS, WHO...  2.79 us
  transfers between devices with their start and end apart: 1, of which 0 were waited for; matrix products, arithmetic and copies ran while one was open for 0% of the time, Pallas kernels for 6%

profile of v4, /device:TPU:1, one launch (start us, length us, event | category | flops | bytes accessed | tf_op | source)
XLA Modules:
  0.0 135.3 jit_solution(6600684796396652656)
XLA Ops:
  0.6 0.0 copy-start.5
  0.6 0.0 copy-start.4
  1.5 2.8 %prepare.1 = (bf16[64,2816]{1,0:T(8,128)(2,1)}, bf16[4,64,256]{2,1,0:T(8,128)(2,1)}, bf16[576,256]{1,0:T(8,128)(2,1)}) custom-call(s32[1]{0:T(128)} %bitcast.dev_ref, s32[128]{0:T(128)} %slot_ref.3, bf16[64,3584]{1,0:T(8,128)(2,1)} %x_ref.1, s32[8,64]{1,0:T(8,128)} %bitcast.38, f32[8,64]{1,0:T(8,128)} %bitcast.39, bf16[16,576,256]{2,1,0:T(8,128)(2,1)} %bitcast.27), custom_call_target="tpu_custom_call" | custom-call | tf_op jit(solution)/shard_map/prepare/pallas_call | solution.py:741
  4.3 0.0 copy-done.5
  4.3 0.0 copy-done.4
  4.3 0.0 copy-start.1
  4.3 0.0 copy-start.2
  4.3 10.8 %conditional.2 = (bf16[576,256]{1,0:T(8,128)(2,1)}, bf16[16,128,512]{2,1,0:T(8,128)(2,1)}) conditional(s32[]{:T(128)} %bitcast.9, (s32[1]{0:T(128)}, s32[2048]{0:T(1024)S(1)}, bf16[16,576,128]{2,1,0:T(8,128)(2,1)S(1)}, bf16[16,576,256]{2,1,0:T(8,128)(2,1)}, bf16[576,256]{1,0:T(8,128)(2,1)}) %tuple.107, ...), branch_computations={%region_0.0_spmd, %region_1.0_spmd, %region_2.0_spmd, %region_3.0_... | conditional | flops 2400000000 | bytes 21769528 | solution.py:706
  4.3 2.1 %collective-permute-start = (bf16[576,256]{1,0:T(8,128)(2,1)}, bf16[576,256]{1,0:T(8,128)(2,1)S(1)}, u32[]{:S(2)}, u32[]{:S(2)}) collective-permute-start(bf16[576,256]{1,0:T(8,128)(2,1)} %get-tuple-element.141), channel_id=1, source_target_pairs={{0,32},{4,36},{8,40},{12,44},{16,48},{20,52},{24,56},{28,60},{32,0... | collective-permute-start | bytes 884744 | tf_op jit(solution)/shard_map/cond/branch_1_fun/ppermute | solution.py:701
  6.4 8.0 %attend.5 = bf16[16,128,512]{2,1,0:T(8,128)(2,1)} custom-call(s32[1]{0:T(128)} %get-tuple-element.142.dev_ref, s32[2048]{0:T(1024)S(1)} %get-tuple-element.143.lens_ref, bf16[16,576,128]{2,1,0:T(8,128)(2,1)S(1)} %get-tuple-element.144.q_ref, bf16[16,576,256]{2,1,0:T(8,128)(2,1)} %get-tuple-element.145.page_ref), custom_call_target="tpu_custom_call" | custom-call | flops 2400000000 | bytes 20000000 | tf_op jit(solution)/shard_map/cond/branch_1_fun/attend/pallas_call | solution.py:652
  14.4 0.0 collective-permute-done
  14.4 0.7 copy.16
  15.1 0.0 copy-done.1
  15.1 0.0 copy-done.2
  15.1 0.0 copy-start.3
  15.1 47.8 %gather_rows.1 = (bf16[4,4,2,64,2816]{4,3,2,1,0:T(8,128)(2,1)S(1)}, bf16[4,4,4,2,64,256]{5,4,3,2,1,0:T(8,128)(2,1)S(1)}, bf16[3,256,1792]{2,1,0:T(8,128)(2,1)}) custom-call(bf16[64,2816]{1,0:T(8,128)(2,1)S(1)} %copy-done.1, bf16[4,64,256]{2,1,0:T(8,128)(2,1)S(1)} %copy-done.2, bf16[3,256,3584]{2,1,0:T(8,128)(2,1)} %wd_hbm.1), custom_call_target="tpu_custom_call" | custom-call | tf_op jit(solution)/shard_map/gather_rows/pallas_call | solution.py:268
  62.9 0.0 copy-done.3
  62.9 0.0 copy-start
  62.9 9.5 %conditional.3 = (bf16[576,256]{1,0:T(8,128)(2,1)}, bf16[3,320,256]{2,1,0:T(8,128)(2,1)S(1)}, bf16[4,512,256]{2,1,0:T(8,128)(2,1)S(1)}) conditional(s32[]{:T(128)} %bitcast.2, (s32[1]{0:T(128)}, bf16[4,512,2816]{2,1,0:T(8,128)(2,1)S(1)}, bf16[4,4,512,256]{3,2,1,0:T(8,128)(2,1)S(1)}, ...), branch_computations={%region_4.0_spmd, %region_5.0_spmd, %region_6.0_spmd, %region_7.0_... | conditional | flops 7000000000 | bytes 31769536 | solution.py:706
  63.0 9.0 %experts_up.8 = (bf16[3,320,256]{2,1,0:T(8,128)(2,1)S(1)}, bf16[4,512,256]{2,1,0:T(8,128)(2,1)S(1)}) custom-call(s32[1]{0:T(128)} %get-tuple-element.157.base_ref, bf16[4,512,2816]{2,1,0:T(8,128)(2,1)S(1)} %get-tuple-element.158.x_ref, bf16[4,4,512,256]{3,2,1,0:T(8,128)(2,1)S(1)} %get-tuple-element.159.xp_ref, ...), custom_call_target="tpu_custom_call" | custom-call | flops 7000000000 | bytes 30000000 | tf_op jit(solution)/shard_map/cond/branch_0_fun/experts_up/pallas_call | solution.py:355
  72.4 0.0 copy-done
  72.4 59.4 %combine.1 = bf16[64,896]{1,0:T(8,128)(2,1)S(1)} custom-call(bf16[3,320,256]{2,1,0:T(8,128)(2,1)S(1)} %get-tuple-element.241.inner_ref, bf16[8,256,256]{2,1,0:T(8,128)(2,1)S(1)} %bitcast.37, bf16[3,256,3584]{2,1,0:T(8,128)(2,1)} %wd_hbm.1, bf16[3,256,1792]{2,1,0:T(8,128)(2,1)S(1)} %copy-done), custom_call_target="tpu_custom_call" | custom-call | tf_op jit(solution)/shard_map/combine/pallas_call | solution.py:596
  131.8 2.9 %attend_one.1 = bf16[16,128,512]{2,1,0:T(8,128)(2,1)} custom-call(s32[1]{0:T(128)} %bitcast.dev_ref, s32[128]{0:T(128)} %slot_ref.3, s32[1]{0:T(128)S(6)} %copy.48.mask_ref, s32[2048]{0:T(1024)S(1)} %copy-done.5, bf16[16,576,128]{2,1,0:T(8,128)(2,1)} %bitcast.32, bf16[576,256]{1,0:T(8,128)(2,1)} %get-tuple-element.239.page_ref, ...), custom_call_target="tpu_custom_call", output_to_operand_aliasing={{}: (6, {})} | custom-call | tf_op jit(solution)/shard_map/attend_one/pallas_call | solution.py:677
  134.7 0.6 copy.49
Async XLA Ops:
  0.6 3.6 %copy-start.5 = (s32[2048]{0:T(1024)S(1)}, s32[2048]{0:T(1024)}, u32[]{:S(2)}) copy-start(s32[2048]{0:T(1024)} %lens_ref.1) | copy-start | bytes 24580
  0.6 3.6 %copy-start.4 = (bf16[16,128,576]{1,2,0:T(8,128)(2,1)S(1)}, bf16[16,128,576]{1,2,0:T(8,128)(2,1)}, u32[]{:S(2)}) copy-start(bf16[16,128,576]{1,2,0:T(8,128)(2,1)} %param.24) | copy-start | bytes 7077892
  4.3 10.9 %copy-start.1 = (bf16[64,2816]{1,0:T(8,128)(2,1)S(1)}, bf16[64,2816]{1,0:T(8,128)(2,1)}, u32[]{:S(2)}) copy-start(bf16[64,2816]{1,0:T(8,128)(2,1)} %get-tuple-element.233.x_ref) | copy-start | bytes 1081348
  4.3 10.9 %copy-start.2 = (bf16[4,64,256]{2,1,0:T(8,128)(2,1)S(1)}, bf16[4,64,256]{2,1,0:T(8,128)(2,1)}, u32[]{:S(2)}) copy-start(bf16[4,64,256]{2,1,0:T(8,128)(2,1)} %get-tuple-element.234.xp_ref) | copy-start | bytes 393220
  4.3 10.1 %collective-permute-start = (bf16[576,256]{1,0:T(8,128)(2,1)}, bf16[576,256]{1,0:T(8,128)(2,1)S(1)}, u32[]{:S(2)}, u32[]{:S(2)}) collective-permute-start(bf16[576,256]{1,0:T(8,128)(2,1)} %get-tuple-element.141), channel_id=1, source_target_pairs={{0,32},{4,36},{8,40},{12,44},{16,48},{20,52},{24,56},{28,60},{32,0... | collective-permute-start | bytes 884744 | tf_op jit(solution)/shard_map/cond/branch_1_fun/ppermute | solution.py:701
  15.1 47.8 %copy-start.3 = (bf16[3,3584,256]{2,1,0:T(8,128)(2,1)S(1)}, bf16[3,3584,256]{2,1,0:T(8,128)(2,1)}, u32[]{:S(2)}) copy-start(bf16[3,3584,256]{2,1,0:T(8,128)(2,1)} %param.31) | copy-start | bytes 16515076
  62.9 9.5 %copy-start = (bf16[3,256,1792]{2,1,0:T(8,128)(2,1)S(1)}, bf16[3,256,1792]{2,1,0:T(8,128)(2,1)}, u32[]{:S(2)}) copy-start(bf16[3,256,1792]{2,1,0:T(8,128)(2,1)} %get-tuple-element.243.wdp_hbm) | copy-start | bytes 8257540

commit v5 on v4

--- a/solution.py
+++ b/solution.py
@@ -414,7 +414,7 @@
     swap = ship(inner_ref, inner2, other, isem.at[0], isem.at[1])
 
     def down(core, source):
-        @pl.loop(0, EXL)
+        @pl.loop(0, EXL, unroll=EXL)
         def _(e):
             row = pl.multiple_of((core * EXL + e) * GSLOT, 8)
             for n in range(2):
@@ -430,7 +430,7 @@
     down(1 - c, inner2)
 
     def scatter(col, start, count):
-        @pl.loop(0, 2 * count, unroll=2)
+        @pl.loop(0, 2 * count, unroll=4 if count == 4 else 2)
         def _(i):
             q = wrap(x + start + i // 2) * 2 + lax.rem(i, 2)
             named = jnp.dot(meta[q, :, 0:128], lanes, preferred_element_type=F32)

time: 136 us -> 135 us (level)
  no operation moved by 1% of the time
where the time goes in v5:
time: 135 us
  Pallas kernels  129 us (96%)
  starting transfers between devices  2.11 us (2%)
  between operations  1.53 us (1%)
  local copies, waits for them, and re-layouts  1.38 us (1%)
    pallas_call x1, Pallas kernels, combine(): pl.pallas_call(combine_kernel, out_shape=jax.ShapeDtypeStruct((ROWS, BLK)...  58.9 us
    pallas_call x1, Pallas kernels, gather_rows(): pl.pallas_call(gather_kernel, out_shape=(jax.ShapeDtypeStruct((4, 4, 2, R...  47.8 us
    pallas_call x1, Pallas kernels, experts_up(): pl.pallas_call(up_kernel, out_shape=(jax.ShapeDtypeStruct((EXL, GROUPS *...  9.02 us
    pallas_call x1, Pallas kernels, attend(): pl.pallas_call(attend_kernel, out_shape=jax.ShapeDtypeStruct((count, head...  8 us
    pallas_call x1, Pallas kernels, attend_one(): pl.pallas_call(attend_one_kernel, out_shape=jax.ShapeDtypeStruct(attended...  2.88 us
    pallas_call x1, Pallas kernels, prepare(): pl.pallas_call(prepare_kernel, out_shape=(jax.ShapeDtypeStruct((ROWS, WHO...  2.79 us
  transfers between devices with their start and end apart: 1, of which 0 were waited for; matrix products, arithmetic and copies ran while one was open for 0% of the time, Pallas kernels for 6%

profile of v5, /device:TPU:1, one launch (start us, length us, event | category | flops | bytes accessed | tf_op | source)
XLA Modules:
  0.0 134.8 jit_solution(11859138900866585513)
XLA Ops:
  0.6 0.0 copy-start.5
  0.6 0.0 copy-start.4
  1.5 2.8 %prepare.1 = (bf16[64,2816]{1,0:T(8,128)(2,1)}, bf16[4,64,256]{2,1,0:T(8,128)(2,1)}, bf16[576,256]{1,0:T(8,128)(2,1)}) custom-call(s32[1]{0:T(128)} %bitcast.dev_ref, s32[128]{0:T(128)} %slot_ref.3, bf16[64,3584]{1,0:T(8,128)(2,1)} %x_ref.1, s32[8,64]{1,0:T(8,128)} %bitcast.38, f32[8,64]{1,0:T(8,128)} %bitcast.39, bf16[16,576,256]{2,1,0:T(8,128)(2,1)} %bitcast.27), custom_call_target="tpu_custom_call" | custom-call | tf_op jit(solution)/shard_map/prepare/pallas_call | solution.py:741
  4.3 0.0 copy-done.5
  4.3 0.0 copy-done.4
  4.3 0.0 copy-start.1
  4.3 0.0 copy-start.2
  4.3 10.8 %conditional.2 = (bf16[576,256]{1,0:T(8,128)(2,1)}, bf16[16,128,512]{2,1,0:T(8,128)(2,1)}) conditional(s32[]{:T(128)} %bitcast.9, (s32[1]{0:T(128)}, s32[2048]{0:T(1024)S(1)}, bf16[16,576,128]{2,1,0:T(8,128)(2,1)S(1)}, bf16[16,576,256]{2,1,0:T(8,128)(2,1)}, bf16[576,256]{1,0:T(8,128)(2,1)}) %tuple.107, ...), branch_computations={%region_0.0_spmd, %region_1.0_spmd, %region_2.0_spmd, %region_3.0_... | conditional | flops 2400000000 | bytes 21769528 | solution.py:706
  4.3 2.1 %collective-permute-start = (bf16[576,256]{1,0:T(8,128)(2,1)}, bf16[576,256]{1,0:T(8,128)(2,1)S(1)}, u32[]{:S(2)}, u32[]{:S(2)}) collective-permute-start(bf16[576,256]{1,0:T(8,128)(2,1)} %get-tuple-element.141), channel_id=1, source_target_pairs={{0,32},{4,36},{8,40},{12,44},{16,48},{20,52},{24,56},{28,60},{32,0... | collective-permute-start | bytes 884744 | tf_op jit(solution)/shard_map/cond/branch_1_fun/ppermute | solution.py:701
  6.4 8.0 %attend.5 = bf16[16,128,512]{2,1,0:T(8,128)(2,1)} custom-call(s32[1]{0:T(128)} %get-tuple-element.142.dev_ref, s32[2048]{0:T(1024)S(1)} %get-tuple-element.143.lens_ref, bf16[16,576,128]{2,1,0:T(8,128)(2,1)S(1)} %get-tuple-element.144.q_ref, bf16[16,576,256]{2,1,0:T(8,128)(2,1)} %get-tuple-element.145.page_ref), custom_call_target="tpu_custom_call" | custom-call | flops 2400000000 | bytes 20000000 | tf_op jit(solution)/shard_map/cond/branch_1_fun/attend/pallas_call | solution.py:652
  14.4 0.0 collective-permute-done
  14.4 0.7 copy.16
  15.1 0.0 copy-done.1
  15.1 0.0 copy-done.2
  15.1 0.0 copy-start.3
  15.1 47.8 %gather_rows.1 = (bf16[4,4,2,64,2816]{4,3,2,1,0:T(8,128)(2,1)S(1)}, bf16[4,4,4,2,64,256]{5,4,3,2,1,0:T(8,128)(2,1)S(1)}, bf16[3,256,1792]{2,1,0:T(8,128)(2,1)}) custom-call(bf16[64,2816]{1,0:T(8,128)(2,1)S(1)} %copy-done.1, bf16[4,64,256]{2,1,0:T(8,128)(2,1)S(1)} %copy-done.2, bf16[3,256,3584]{2,1,0:T(8,128)(2,1)} %wd_hbm.1), custom_call_target="tpu_custom_call" | custom-call | tf_op jit(solution)/shard_map/gather_rows/pallas_call | solution.py:268
  62.9 0.0 copy-done.3
  62.9 0.0 copy-start
  62.9 9.5 %conditional.3 = (bf16[576,256]{1,0:T(8,128)(2,1)}, bf16[3,320,256]{2,1,0:T(8,128)(2,1)S(1)}, bf16[4,512,256]{2,1,0:T(8,128)(2,1)S(1)}) conditional(s32[]{:T(128)} %bitcast.2, (s32[1]{0:T(128)}, bf16[4,512,2816]{2,1,0:T(8,128)(2,1)S(1)}, bf16[4,4,512,256]{3,2,1,0:T(8,128)(2,1)S(1)}, ...), branch_computations={%region_4.0_spmd, %region_5.0_spmd, %region_6.0_spmd, %region_7.0_... | conditional | flops 7000000000 | bytes 31769536 | solution.py:706
  63.0 9.0 %experts_up.8 = (bf16[3,320,256]{2,1,0:T(8,128)(2,1)S(1)}, bf16[4,512,256]{2,1,0:T(8,128)(2,1)S(1)}) custom-call(s32[1]{0:T(128)} %get-tuple-element.157.base_ref, bf16[4,512,2816]{2,1,0:T(8,128)(2,1)S(1)} %get-tuple-element.158.x_ref, bf16[4,4,512,256]{3,2,1,0:T(8,128)(2,1)S(1)} %get-tuple-element.159.xp_ref, ...), custom_call_target="tpu_custom_call" | custom-call | flops 7000000000 | bytes 30000000 | tf_op jit(solution)/shard_map/cond/branch_0_fun/experts_up/pallas_call | solution.py:355
  72.4 0.0 copy-done
  72.4 58.9 %combine.1 = bf16[64,896]{1,0:T(8,128)(2,1)S(1)} custom-call(bf16[3,320,256]{2,1,0:T(8,128)(2,1)S(1)} %get-tuple-element.241.inner_ref, bf16[8,256,256]{2,1,0:T(8,128)(2,1)S(1)} %bitcast.37, bf16[3,256,3584]{2,1,0:T(8,128)(2,1)} %wd_hbm.1, bf16[3,256,1792]{2,1,0:T(8,128)(2,1)S(1)} %copy-done), custom_call_target="tpu_custom_call" | custom-call | tf_op jit(solution)/shard_map/combine/pallas_call | solution.py:596
  131.3 2.9 %attend_one.1 = bf16[16,128,512]{2,1,0:T(8,128)(2,1)} custom-call(s32[1]{0:T(128)} %bitcast.dev_ref, s32[128]{0:T(128)} %slot_ref.3, s32[1]{0:T(128)S(6)} %copy.48.mask_ref, s32[2048]{0:T(1024)S(1)} %copy-done.5, bf16[16,576,128]{2,1,0:T(8,128)(2,1)} %bitcast.32, bf16[576,256]{1,0:T(8,128)(2,1)} %get-tuple-element.239.page_ref, ...), custom_call_target="tpu_custom_call", output_to_operand_aliasing={{}: (6, {})} | custom-call | tf_op jit(solution)/shard_map/attend_one/pallas_call | solution.py:677
  134.2 0.6 copy.49
Async XLA Ops:
  0.6 3.6 %copy-start.5 = (s32[2048]{0:T(1024)S(1)}, s32[2048]{0:T(1024)}, u32[]{:S(2)}) copy-start(s32[2048]{0:T(1024)} %lens_ref.1) | copy-start | bytes 24580
  0.6 3.6 %copy-start.4 = (bf16[16,128,576]{1,2,0:T(8,128)(2,1)S(1)}, bf16[16,128,576]{1,2,0:T(8,128)(2,1)}, u32[]{:S(2)}) copy-start(bf16[16,128,576]{1,2,0:T(8,128)(2,1)} %param.24) | copy-start | bytes 7077892
  4.3 10.9 %copy-start.1 = (bf16[64,2816]{1,0:T(8,128)(2,1)S(1)}, bf16[64,2816]{1,0:T(8,128)(2,1)}, u32[]{:S(2)}) copy-start(bf16[64,2816]{1,0:T(8,128)(2,1)} %get-tuple-element.233.x_ref) | copy-start | bytes 1081348
  4.3 10.9 %copy-start.2 = (bf16[4,64,256]{2,1,0:T(8,128)(2,1)S(1)}, bf16[4,64,256]{2,1,0:T(8,128)(2,1)}, u32[]{:S(2)}) copy-start(bf16[4,64,256]{2,1,0:T(8,128)(2,1)} %get-tuple-element.234.xp_ref) | copy-start | bytes 393220
  4.3 10.1 %collective-permute-start = (bf16[576,256]{1,0:T(8,128)(2,1)}, bf16[576,256]{1,0:T(8,128)(2,1)S(1)}, u32[]{:S(2)}, u32[]{:S(2)}) collective-permute-start(bf16[576,256]{1,0:T(8,128)(2,1)} %get-tuple-element.141), channel_id=1, source_target_pairs={{0,32},{4,36},{8,40},{12,44},{16,48},{20,52},{24,56},{28,60},{32,0... | collective-permute-start | bytes 884744 | tf_op jit(solution)/shard_map/cond/branch_1_fun/ppermute | solution.py:701
  15.1 47.8 %copy-start.3 = (bf16[3,3584,256]{2,1,0:T(8,128)(2,1)S(1)}, bf16[3,3584,256]{2,1,0:T(8,128)(2,1)}, u32[]{:S(2)}) copy-start(bf16[3,3584,256]{2,1,0:T(8,128)(2,1)} %param.31) | copy-start | bytes 16515076
  62.9 9.5 %copy-start = (bf16[3,256,1792]{2,1,0:T(8,128)(2,1)S(1)}, bf16[3,256,1792]{2,1,0:T(8,128)(2,1)}, u32[]{:S(2)}) copy-start(bf16[3,256,1792]{2,1,0:T(8,128)(2,1)} %get-tuple-element.243.wdp_hbm) | copy-start | bytes 8257540

commit v6 on v5

--- a/solution.py
+++ b/solution.py
@@ -323,7 +323,7 @@
     want = slot_numbers((EXL * PSLOT, PAIR), 0, PSLOT)
     lanes = expert_lanes((EXL * PSLOT, 128), 0, base_ref[0], PSLOT)
 
-    @pl.loop(0, GROUPS // 2)
+    @pl.loop(0, GROUPS // 2, unroll=2)
     def _(q):
         table = x_ref[q, :, MAIN : MAIN + 128]
         named = lax.dot_general(lanes, table, (((1,), (1,)), ((), ())), preferred_element_type=F32)

time: 135 us -> 143 us (1.059)
  loops' own time: 0.48 us -> 8.63 us
    another operation x2, loops' own time: 0.48 us -> 8.63 us  [trade(): return lax.switch(bits, [branch(m) for m in range(steps)], page)]
where the time goes in v6:
time: 143 us
  Pallas kernels  129 us (90%)
  loops' own time  8.63 us (6%)
  starting transfers between devices  2.11 us (1%)
  between operations  1.53 us (1%)
    pallas_call x1, Pallas kernels, combine(): pl.pallas_call(combine_kernel, out_shape=jax.ShapeDtypeStruct((ROWS, BLK)...  58.9 us
    pallas_call x1, Pallas kernels, gather_rows(): pl.pallas_call(gather_kernel, out_shape=(jax.ShapeDtypeStruct((4, 4, 2, R...  47.8 us
    pallas_call x1, Pallas kernels, experts_up(): pl.pallas_call(up_kernel, out_shape=(jax.ShapeDtypeStruct((EXL, GROUPS *...  8.73 us
    another operation x2, loops' own time, trade(): return lax.switch(bits, [branch(m) for m in range(steps)], page)  8.63 us
    pallas_call x1, Pallas kernels, attend(): pl.pallas_call(attend_kernel, out_shape=jax.ShapeDtypeStruct((count, head...  8 us
    pallas_call x1, Pallas kernels, attend_one(): pl.pallas_call(attend_one_kernel, out_shape=jax.ShapeDtypeStruct(attended...  2.88 us
  transfers between devices with their start and end apart: 1, of which 0 were waited for; matrix products, arithmetic and copies ran while one was open for 0% of the time, Pallas kernels for 6%

profile of v6, /device:TPU:1, one launch (start us, length us, event | category | flops | bytes accessed | tf_op | source)
XLA Modules:
  0.0 142.7 jit_solution(16456459226117952303)
XLA Ops:
  0.6 0.0 copy-start.5
  0.6 0.0 copy-start.4
  1.5 2.8 %prepare.1 = (bf16[64,2816]{1,0:T(8,128)(2,1)}, bf16[4,64,256]{2,1,0:T(8,128)(2,1)}, bf16[576,256]{1,0:T(8,128)(2,1)}) custom-call(s32[1]{0:T(128)} %bitcast.dev_ref, s32[128]{0:T(128)} %slot_ref.3, bf16[64,3584]{1,0:T(8,128)(2,1)} %x_ref.1, s32[8,64]{1,0:T(8,128)} %bitcast.38, f32[8,64]{1,0:T(8,128)} %bitcast.39, bf16[16,576,256]{2,1,0:T(8,128)(2,1)} %bitcast.27), custom_call_target="tpu_custom_call" | custom-call | tf_op jit(solution)/shard_map/prepare/pallas_call | solution.py:741
  4.3 0.0 copy-done.5
  4.3 0.0 copy-done.4
  4.3 0.0 copy-start.1
  4.3 0.0 copy-start.2
  4.3 10.8 %conditional.2 = (bf16[576,256]{1,0:T(8,128)(2,1)}, bf16[16,128,512]{2,1,0:T(8,128)(2,1)}) conditional(s32[]{:T(128)} %bitcast.9, (s32[1]{0:T(128)}, s32[2048]{0:T(1024)S(1)}, bf16[16,576,128]{2,1,0:T(8,128)(2,1)S(1)}, bf16[16,576,256]{2,1,0:T(8,128)(2,1)}, bf16[576,256]{1,0:T(8,128)(2,1)}) %tuple.107, ...), branch_computations={%region_0.0_spmd, %region_1.0_spmd, %region_2.0_spmd, %region_3.0_... | conditional | flops 2400000000 | bytes 21769528 | solution.py:706
  4.3 2.1 %collective-permute-start = (bf16[576,256]{1,0:T(8,128)(2,1)}, bf16[576,256]{1,0:T(8,128)(2,1)S(1)}, u32[]{:S(2)}, u32[]{:S(2)}) collective-permute-start(bf16[576,256]{1,0:T(8,128)(2,1)} %get-tuple-element.141), channel_id=1, source_target_pairs={{0,32},{4,36},{8,40},{12,44},{16,48},{20,52},{24,56},{28,60},{32,0... | collective-permute-start | bytes 884744 | tf_op jit(solution)/shard_map/cond/branch_1_fun/ppermute | solution.py:701
  6.4 8.0 %attend.5 = bf16[16,128,512]{2,1,0:T(8,128)(2,1)} custom-call(s32[1]{0:T(128)} %get-tuple-element.142.dev_ref, s32[2048]{0:T(1024)S(1)} %get-tuple-element.143.lens_ref, bf16[16,576,128]{2,1,0:T(8,128)(2,1)S(1)} %get-tuple-element.144.q_ref, bf16[16,576,256]{2,1,0:T(8,128)(2,1)} %get-tuple-element.145.page_ref), custom_call_target="tpu_custom_call" | custom-call | flops 2400000000 | bytes 20000000 | tf_op jit(solution)/shard_map/cond/branch_1_fun/attend/pallas_call | solution.py:652
  14.4 0.0 collective-permute-done
  14.4 0.7 copy.16
  15.1 0.0 copy-done.1
  15.1 0.0 copy-done.2
  15.1 0.0 copy-start.3
  15.1 47.8 %gather_rows.1 = (bf16[4,4,2,64,2816]{4,3,2,1,0:T(8,128)(2,1)S(1)}, bf16[4,4,4,2,64,256]{5,4,3,2,1,0:T(8,128)(2,1)S(1)}, bf16[3,256,1792]{2,1,0:T(8,128)(2,1)}) custom-call(bf16[64,2816]{1,0:T(8,128)(2,1)S(1)} %copy-done.1, bf16[4,64,256]{2,1,0:T(8,128)(2,1)S(1)} %copy-done.2, bf16[3,256,3584]{2,1,0:T(8,128)(2,1)} %wd_hbm.1), custom_call_target="tpu_custom_call" | custom-call | tf_op jit(solution)/shard_map/gather_rows/pallas_call | solution.py:268
  62.9 0.0 copy-done.3
  62.9 0.0 copy-start
  62.9 17.3 %conditional.3 = (bf16[576,256]{1,0:T(8,128)(2,1)}, bf16[3,320,256]{2,1,0:T(8,128)(2,1)S(1)}, bf16[4,512,256]{2,1,0:T(8,128)(2,1)S(1)}) conditional(s32[]{:T(128)} %bitcast.2, (s32[1]{0:T(128)}, bf16[4,512,2816]{2,1,0:T(8,128)(2,1)S(1)}, bf16[4,4,512,256]{3,2,1,0:T(8,128)(2,1)S(1)}, ...), branch_computations={%region_4.0_spmd, %region_5.0_spmd, %region_6.0_spmd, %region_7.0_... | conditional | flops 7000000000 | bytes 31769536 | solution.py:706
  63.0 8.7 %experts_up.8 = (bf16[3,320,256]{2,1,0:T(8,128)(2,1)S(1)}, bf16[4,512,256]{2,1,0:T(8,128)(2,1)S(1)}) custom-call(s32[1]{0:T(128)} %get-tuple-element.157.base_ref, bf16[4,512,2816]{2,1,0:T(8,128)(2,1)S(1)} %get-tuple-element.158.x_ref, bf16[4,4,512,256]{3,2,1,0:T(8,128)(2,1)S(1)} %get-tuple-element.159.xp_ref, ...), custom_call_target="tpu_custom_call" | custom-call | flops 7000000000 | bytes 30000000 | tf_op jit(solution)/shard_map/cond/branch_0_fun/experts_up/pallas_call | solution.py:355
  80.3 0.0 copy-done
  80.3 58.9 %combine.1 = bf16[64,896]{1,0:T(8,128)(2,1)S(1)} custom-call(bf16[3,320,256]{2,1,0:T(8,128)(2,1)S(1)} %get-tuple-element.241.inner_ref, bf16[8,256,256]{2,1,0:T(8,128)(2,1)S(1)} %bitcast.37, bf16[3,256,3584]{2,1,0:T(8,128)(2,1)} %wd_hbm.1, bf16[3,256,1792]{2,1,0:T(8,128)(2,1)S(1)} %copy-done), custom_call_target="tpu_custom_call" | custom-call | tf_op jit(solution)/shard_map/combine/pallas_call | solution.py:596
  139.2 2.9 %attend_one.1 = bf16[16,128,512]{2,1,0:T(8,128)(2,1)} custom-call(s32[1]{0:T(128)} %bitcast.dev_ref, s32[128]{0:T(128)} %slot_ref.3, s32[1]{0:T(128)S(6)} %copy.48.mask_ref, s32[2048]{0:T(1024)S(1)} %copy-done.5, bf16[16,576,128]{2,1,0:T(8,128)(2,1)} %bitcast.32, bf16[576,256]{1,0:T(8,128)(2,1)} %get-tuple-element.239.page_ref, ...), custom_call_target="tpu_custom_call", output_to_operand_aliasing={{}: (6, {})} | custom-call | tf_op jit(solution)/shard_map/attend_one/pallas_call | solution.py:677
  142.0 0.6 copy.49
Async XLA Ops:
  0.6 3.6 %copy-start.5 = (s32[2048]{0:T(1024)S(1)}, s32[2048]{0:T(1024)}, u32[]{:S(2)}) copy-start(s32[2048]{0:T(1024)} %lens_ref.1) | copy-start | bytes 24580
  0.6 3.6 %copy-start.4 = (bf16[16,128,576]{1,2,0:T(8,128)(2,1)S(1)}, bf16[16,128,576]{1,2,0:T(8,128)(2,1)}, u32[]{:S(2)}) copy-start(bf16[16,128,576]{1,2,0:T(8,128)(2,1)} %param.24) | copy-start | bytes 7077892
  4.3 10.9 %copy-start.1 = (bf16[64,2816]{1,0:T(8,128)(2,1)S(1)}, bf16[64,2816]{1,0:T(8,128)(2,1)}, u32[]{:S(2)}) copy-start(bf16[64,2816]{1,0:T(8,128)(2,1)} %get-tuple-element.233.x_ref) | copy-start | bytes 1081348
  4.3 10.9 %copy-start.2 = (bf16[4,64,256]{2,1,0:T(8,128)(2,1)S(1)}, bf16[4,64,256]{2,1,0:T(8,128)(2,1)}, u32[]{:S(2)}) copy-start(bf16[4,64,256]{2,1,0:T(8,128)(2,1)} %get-tuple-element.234.xp_ref) | copy-start | bytes 393220
  4.3 10.1 %collective-permute-start = (bf16[576,256]{1,0:T(8,128)(2,1)}, bf16[576,256]{1,0:T(8,128)(2,1)S(1)}, u32[]{:S(2)}, u32[]{:S(2)}) collective-permute-start(bf16[576,256]{1,0:T(8,128)(2,1)} %get-tuple-element.141), channel_id=1, source_target_pairs={{0,32},{4,36},{8,40},{12,44},{16,48},{20,52},{24,56},{28,60},{32,0... | collective-permute-start | bytes 884744 | tf_op jit(solution)/shard_map/cond/branch_1_fun/ppermute | solution.py:701
  15.1 47.8 %copy-start.3 = (bf16[3,3584,256]{2,1,0:T(8,128)(2,1)S(1)}, bf16[3,3584,256]{2,1,0:T(8,128)(2,1)}, u32[]{:S(2)}) copy-start(bf16[3,3584,256]{2,1,0:T(8,128)(2,1)} %param.31) | copy-start | bytes 16515076
  62.9 17.4 %copy-start = (bf16[3,256,1792]{2,1,0:T(8,128)(2,1)S(1)}, bf16[3,256,1792]{2,1,0:T(8,128)(2,1)}, u32[]{:S(2)}) copy-start(bf16[3,256,1792]{2,1,0:T(8,128)(2,1)} %get-tuple-element.243.wdp_hbm) | copy-start | bytes 8257540
